TPU v7x, 32 devices: a whole 2x2x4 slice. The times are simulated.
32 devices in a mesh: seq: 4 (over y, x), fsdp: 8 (over z, core).
Axes of the slice: x: 2, y: 2, z: 4, core: 2. Of those that a mesh axis runs over, the one named last changes fastest.
Arguments:
- tokens: bfloat16 [8, 2048, 1024], P('fsdp', 'seq'), may hold values from -6 to 6
- block_ids: int32 [8, 2048], P('fsdp'), may hold values from 0 to 7, never falling along the last dimension, each value on 1 to 512 neighbouring positions
- gain_attn: bfloat16 [1024], P('fsdp'), may hold values from 0.5 to 1.5
- w_query: bfloat16 [1024, 1024], P('fsdp'), may hold values from -0.25 to 0.25
- w_latent: bfloat16 [1024, 512], P('fsdp'), may hold values from -0.1875 to 0.1875
- up_key: bfloat16 [2, 256, 512], P(None, 'fsdp'), may hold values from -0.375 to 0.375
- up_value: bfloat16 [2, 256, 512], P(None, 'fsdp'), may hold values from -0.375 to 0.375
- w_out: bfloat16 [1024, 1024], P('fsdp'), may hold values from -3 to 3
- gain_ffn: bfloat16 [1024], P('fsdp'), may hold values from 0.5 to 1.5
- w_gate: bfloat16 [1024, 2816], P('fsdp'), may hold values from -0.1875 to 0.1875
- w_up: bfloat16 [1024, 2816], P('fsdp'), may hold values from -0.1875 to 0.1875
- w_down: bfloat16 [2816, 1024], P('fsdp'), may hold values from -0.109375 to 0.109375
- cotangent: bfloat16 [8, 2048, 1024], P('fsdp', 'seq'), may hold values from -6 to 6
Outputs:
- mixed_out: bfloat16 [8, 2048, 1024], P('fsdp', 'seq')
- grad_tokens: float32 [8, 2048, 1024], P('fsdp', 'seq')
- grad_gain_attn: float32 [1024], P('fsdp')
- grad_w_query: float32 [1024, 1024], P('fsdp')
- grad_w_latent: float32 [1024, 512], P('fsdp')
- grad_up_key: float32 [2, 256, 512], P(None, 'fsdp')
- grad_up_value: float32 [2, 256, 512], P(None, 'fsdp')
- grad_w_out: float32 [1024, 1024], P('fsdp')
- grad_gain_ffn: float32 [1024], P('fsdp')
- grad_w_gate: float32 [1024, 2816], P('fsdp')
- grad_w_up: float32 [1024, 2816], P('fsdp')
- grad_w_down: float32 [2816, 1024], P('fsdp')
Inputs may be any that keep to these rules, and one draw needn't show every extreme that they name: `block_ids`: within each sequence the block ids never fall, start at 0, and each block spans 1 to 512 tokens.
All inputs are finite; a program needn't handle non-finite values.
Results may differ from a plain program's by a relative error of at most 0.02.
Values may be sent and summed in bfloat16 or wider, within the bound.
A program may use at most 256 MiB of HBM per device.

v0:
```python
import jax
import jax.numpy as jnp
from jax import lax
from jax.sharding import PartitionSpec as P

HEADS = 16
HEAD = 64
GROUPS = 2
LATENT = 256


EPSILON = 1e-05
HIGH = lax.Precision.HIGHEST


def normalize(values):
    inverse = lax.rsqrt(jnp.mean(values * values, axis=-1, keepdims=True) + EPSILON)
    return (values * inverse, inverse)


def norm_back(grad_normed, normed, inverse):
    return inverse * (grad_normed - normed * jnp.mean(grad_normed * normed, axis=-1, keepdims=True))


def lift_heads(latent, up_key, up_value):
    count = latent.shape[0]
    grouped = latent.reshape(count, GROUPS, LATENT)
    key_part = jnp.einsum("ngr,grc->ngc", grouped, up_key, preferred_element_type=jnp.float32)
    value_part = jnp.einsum("ngr,grc->ngc", grouped, up_value, preferred_element_type=jnp.float32)
    return (
        key_part.astype(jnp.bfloat16).reshape(count, -1),
        value_part.astype(jnp.bfloat16).reshape(count, -1),
    )


def lower_grads(key_grad, value_grad, up_key, up_value):
    count = key_grad.shape[0]
    key_grouped = key_grad.reshape(count, GROUPS, -1)
    value_grouped = value_grad.reshape(count, GROUPS, -1)
    return (
        jnp.einsum("ngc,grc->ngr", key_grouped, up_key.astype(jnp.float32), precision=HIGH)
        + jnp.einsum("ngc,grc->ngr", value_grouped, up_value.astype(jnp.float32), precision=HIGH)
    ).reshape(count, -1)


def up_grads(latent, key_grad, value_grad):
    count = key_grad.shape[0]
    grouped = latent.astype(jnp.float32).reshape(count, GROUPS, LATENT)
    grad_key_up = jnp.einsum(
        "ngr,ngc->grc", grouped, key_grad.reshape(count, GROUPS, -1), precision=HIGH
    )
    grad_value_up = jnp.einsum(
        "ngr,ngc->grc", grouped, value_grad.reshape(count, GROUPS, -1), precision=HIGH
    )
    return (grad_key_up, grad_value_up)


def split_heads(values):
    return values.reshape(values.shape[0], HEADS, HEAD).transpose(1, 0, 2)


def merge_heads(values):
    return values.transpose(1, 0, 2).reshape(values.shape[1], HEADS * HEAD)


def local(
    tokens,
    block_ids,
    gain_attn,
    w_query,
    w_latent,
    up_key,
    up_value,
    w_out,
    gain_ffn,
    w_gate,
    w_up,
    w_down,
    cotangent,
):
    count = tokens.shape[1]
    scale = HEAD ** (-0.5)
    gain_one, query_full, latent_full, out_full, key_up, value_up = (
        lax.all_gather(gain_attn, "fsdp", axis=0, tiled=True),
        lax.all_gather(w_query, "fsdp", axis=0, tiled=True),
        lax.all_gather(w_latent, "fsdp", axis=0, tiled=True),
        lax.all_gather(w_out, "fsdp", axis=0, tiled=True),
        lax.all_gather(up_key, "fsdp", axis=1, tiled=True),
        lax.all_gather(up_value, "fsdp", axis=1, tiled=True),
    )
    gain_two, gate_full, upper_full, down_full = (
        lax.all_gather(gain_ffn, "fsdp", axis=0, tiled=True),
        lax.all_gather(w_gate, "fsdp", axis=0, tiled=True),
        lax.all_gather(w_up, "fsdp", axis=0, tiled=True),
        lax.all_gather(w_down, "fsdp", axis=0, tiled=True),
    )
    inputs = tokens[0].astype(jnp.float32)
    normed_one, inverse_one = normalize(inputs)
    hidden_one = (normed_one * gain_one.astype(jnp.float32)).astype(jnp.bfloat16)
    query = jnp.dot(hidden_one, query_full, preferred_element_type=jnp.float32).astype(jnp.bfloat16)
    latent = jnp.dot(hidden_one, latent_full, preferred_element_type=jnp.float32).astype(
        jnp.bfloat16
    )
    key_ids = block_ids[0]
    query_ids = lax.dynamic_slice_in_dim(key_ids, lax.axis_index("seq") * count, count)
    allowed = key_ids[None, :] <= query_ids[:, None]
    own_keys, own_values = lift_heads(latent, key_up, value_up)
    key_all, value_all = (
        lax.all_gather(own_keys, "seq", axis=0, tiled=True),
        lax.all_gather(own_values, "seq", axis=0, tiled=True),
    )
    query_heads = split_heads(query)
    key_heads = split_heads(key_all)
    value_heads = split_heads(value_all)

    def masked_scores(query_head, key_head):
        raw = (
            jnp.einsum("qd,kd->qk", query_head, key_head, preferred_element_type=jnp.float32)
            * scale
        )
        return jnp.where(allowed, raw, -1e30)

    def forward_head(pieces):
        query_head, key_head, value_head = pieces
        scores = masked_scores(query_head, key_head)
        peak = jnp.max(scores, axis=-1, keepdims=True)
        shifted = jnp.exp(scores - peak)
        total = jnp.sum(shifted, axis=-1, keepdims=True)
        probs = (shifted / total).astype(jnp.bfloat16)
        return (
            jnp.dot(probs, value_head, preferred_element_type=jnp.float32),
            (peak + jnp.log(total))[:, 0],
        )

    head_out, log_totals = lax.map(forward_head, (query_heads, key_heads, value_heads))
    mixed = merge_heads(head_out).astype(jnp.bfloat16)
    resid = inputs + jnp.dot(mixed, out_full, preferred_element_type=jnp.float32)
    normed_two, inverse_two = normalize(resid)
    hidden_two = (normed_two * gain_two.astype(jnp.float32)).astype(jnp.bfloat16)
    gate_proj = jnp.dot(hidden_two, gate_full, preferred_element_type=jnp.float32)
    up_proj = jnp.dot(hidden_two, upper_full, preferred_element_type=jnp.float32)
    sigma = jax.nn.sigmoid(gate_proj)
    hidden = (gate_proj * sigma * up_proj).astype(jnp.bfloat16)
    output = resid + jnp.dot(hidden, down_full, preferred_element_type=jnp.float32)
    gain_two, gate_full, upper_full, down_full = (
        lax.all_gather(gain_ffn, "fsdp", axis=0, tiled=True),
        lax.all_gather(w_gate, "fsdp", axis=0, tiled=True),
        lax.all_gather(w_up, "fsdp", axis=0, tiled=True),
        lax.all_gather(w_down, "fsdp", axis=0, tiled=True),
    )
    grad_out = cotangent[0]
    d_hidden = (
        jnp.einsum("td,fd->tf", grad_out, down_full, preferred_element_type=jnp.float32)
        .astype(jnp.bfloat16)
        .astype(jnp.float32)
    )
    grad_down = jnp.einsum("tf,td->fd", hidden, grad_out, preferred_element_type=jnp.float32)
    d_gate = (d_hidden * up_proj * sigma * (1.0 + gate_proj * (1.0 - sigma))).astype(jnp.bfloat16)
    d_up = (d_hidden * gate_proj * sigma).astype(jnp.bfloat16)
    grad_gate = jnp.einsum("td,tf->df", hidden_two, d_gate, preferred_element_type=jnp.float32)
    grad_upper = jnp.einsum("td,tf->df", hidden_two, d_up, preferred_element_type=jnp.float32)
    d_hidden_two = jnp.einsum(
        "tf,df->td", d_gate, gate_full, preferred_element_type=jnp.float32
    ) + jnp.einsum("tf,df->td", d_up, upper_full, preferred_element_type=jnp.float32)
    grad_gain_two = jnp.sum(d_hidden_two * normed_two, axis=0)
    d_resid = grad_out.astype(jnp.float32) + norm_back(
        d_hidden_two * gain_two.astype(jnp.float32), normed_two, inverse_two
    )
    gain_one, query_full, latent_full, out_full, key_up, value_up = (
        lax.all_gather(gain_attn, "fsdp", axis=0, tiled=True),
        lax.all_gather(w_query, "fsdp", axis=0, tiled=True),
        lax.all_gather(w_latent, "fsdp", axis=0, tiled=True),
        lax.all_gather(w_out, "fsdp", axis=0, tiled=True),
        lax.all_gather(up_key, "fsdp", axis=1, tiled=True),
        lax.all_gather(up_value, "fsdp", axis=1, tiled=True),
    )
    d_attn = d_resid.astype(jnp.bfloat16)
    grad_out_proj = jnp.einsum("tc,td->cd", mixed, d_attn, preferred_element_type=jnp.float32)
    d_mixed = jnp.einsum("td,cd->tc", d_attn, out_full, preferred_element_type=jnp.float32).astype(
        jnp.bfloat16
    )

    def backward_head(pieces):
        query_head, key_head, value_head, grad_head, log_total = pieces
        scores = masked_scores(query_head, key_head)
        probs = jnp.where(allowed, jnp.exp(scores - log_total[:, None]), 0.0)
        grad_probs = jnp.einsum(
            "qd,kd->qk", grad_head, value_head, preferred_element_type=jnp.float32
        )
        delta = jnp.sum(probs * grad_probs, axis=-1, keepdims=True)
        grad_scores = (probs * (grad_probs - delta)).astype(jnp.bfloat16)
        grad_query = jnp.dot(grad_scores, key_head, preferred_element_type=jnp.float32) * scale
        grad_key = (
            jnp.einsum("qk,qd->kd", grad_scores, query_head, preferred_element_type=jnp.float32)
            * scale
        )
        grad_value = jnp.einsum(
            "qk,qd->kd", probs.astype(jnp.bfloat16), grad_head, preferred_element_type=jnp.float32
        )
        return (grad_query, grad_key, grad_value)

    query_grads, key_grads, value_grads = lax.map(
        backward_head, (query_heads, key_heads, value_heads, split_heads(d_mixed), log_totals)
    )
    key_terms = merge_heads(key_grads)
    value_terms = merge_heads(value_grads)
    key_sum, value_sum = (
        lax.psum_scatter(
            key_terms.astype(jnp.bfloat16), "seq", scatter_dimension=0, tiled=True
        ).astype(jnp.float32),
        lax.psum_scatter(
            value_terms.astype(jnp.bfloat16), "seq", scatter_dimension=0, tiled=True
        ).astype(jnp.float32),
    )
    d_latent = lower_grads(key_sum, value_sum, key_up, value_up).astype(jnp.bfloat16)
    grad_key_up, grad_value_up = up_grads(latent, key_sum, value_sum)
    d_query = merge_heads(query_grads).astype(jnp.bfloat16)
    grad_query = jnp.einsum("td,tc->dc", hidden_one, d_query, preferred_element_type=jnp.float32)
    grad_latent = jnp.einsum("td,tc->dc", hidden_one, d_latent, preferred_element_type=jnp.float32)
    d_hidden_one = jnp.einsum(
        "tc,dc->td", d_query, query_full, preferred_element_type=jnp.float32
    ) + jnp.einsum("tc,dc->td", d_latent, latent_full, preferred_element_type=jnp.float32)
    grad_gain_one = jnp.sum(d_hidden_one * normed_one, axis=0)
    d_inputs = d_resid + norm_back(
        d_hidden_one * gain_one.astype(jnp.float32), normed_one, inverse_one
    )
    part_g1, part_query, part_latent, part_out, part_key, part_value = (
        lax.psum_scatter(
            grad_gain_one.astype(jnp.bfloat16), "fsdp", scatter_dimension=0, tiled=True
        ).astype(jnp.float32),
        lax.psum_scatter(
            grad_query.astype(jnp.bfloat16), "fsdp", scatter_dimension=0, tiled=True
        ).astype(jnp.float32),
        lax.psum_scatter(
            grad_latent.astype(jnp.bfloat16), "fsdp", scatter_dimension=0, tiled=True
        ).astype(jnp.float32),
        lax.psum_scatter(
            grad_out_proj.astype(jnp.bfloat16), "fsdp", scatter_dimension=0, tiled=True
        ).astype(jnp.float32),
        lax.psum_scatter(
            grad_key_up.astype(jnp.bfloat16), "fsdp", scatter_dimension=1, tiled=True
        ).astype(jnp.float32),
        lax.psum_scatter(
            grad_value_up.astype(jnp.bfloat16), "fsdp", scatter_dimension=1, tiled=True
        ).astype(jnp.float32),
    )
    part_g2, part_gate, part_upper, part_down = (
        lax.psum_scatter(
            grad_gain_two.astype(jnp.bfloat16), "fsdp", scatter_dimension=0, tiled=True
        ).astype(jnp.float32),
        lax.psum_scatter(
            grad_gate.astype(jnp.bfloat16), "fsdp", scatter_dimension=0, tiled=True
        ).astype(jnp.float32),
        lax.psum_scatter(
            grad_upper.astype(jnp.bfloat16), "fsdp", scatter_dimension=0, tiled=True
        ).astype(jnp.float32),
        lax.psum_scatter(
            grad_down.astype(jnp.bfloat16), "fsdp", scatter_dimension=0, tiled=True
        ).astype(jnp.float32),
    )
    totals = (
        lax.psum(part_g1.astype(jnp.bfloat16), "seq").astype(jnp.float32),
        lax.psum(part_query.astype(jnp.bfloat16), "seq").astype(jnp.float32),
        lax.psum(part_latent.astype(jnp.bfloat16), "seq").astype(jnp.float32),
        lax.psum(part_key.astype(jnp.bfloat16), "seq").astype(jnp.float32),
        lax.psum(part_value.astype(jnp.bfloat16), "seq").astype(jnp.float32),
        lax.psum(part_out.astype(jnp.bfloat16), "seq").astype(jnp.float32),
        lax.psum(part_g2.astype(jnp.bfloat16), "seq").astype(jnp.float32),
        lax.psum(part_gate.astype(jnp.bfloat16), "seq").astype(jnp.float32),
        lax.psum(part_upper.astype(jnp.bfloat16), "seq").astype(jnp.float32),
        lax.psum(part_down.astype(jnp.bfloat16), "seq").astype(jnp.float32),
    )
    return (
        output.astype(jnp.bfloat16)[None],
        d_inputs[None],
        totals[0],
        totals[1],
        totals[2],
        totals[3],
        totals[4],
        totals[5],
        totals[6],
        totals[7],
        totals[8],
        totals[9],
    )


def solution(mesh):
    placed = (
        P("fsdp", "seq", None),
        P("fsdp", None),
        P("fsdp"),
        P("fsdp", None),
        P("fsdp", None),
        P(None, "fsdp", None),
        P(None, "fsdp", None),
        P("fsdp", None),
        P("fsdp"),
        P("fsdp", None),
        P("fsdp", None),
        P("fsdp", None),
        P("fsdp", "seq", None),
    )
    return jax.shard_map(
        local,
        mesh=mesh,
        in_specs=placed,
        out_specs=(
            P("fsdp", "seq", None),
            P("fsdp", "seq", None),
            P("fsdp"),
            P("fsdp", None),
            P("fsdp", None),
            P(None, "fsdp", None),
            P(None, "fsdp", None),
            P("fsdp", None),
            P("fsdp"),
            P("fsdp", None),
            P("fsdp", None),
            P("fsdp", None),
        ),
        check_vma=False,
    )
```

profile of v0, /device:TPU:0, one launch (start us, length us, event | category | flops | bytes accessed | tf_op | source)
XLA Modules:
  0.0 1191.2 jit_solution(1598894832321759793)
XLA Ops:
  8.7 13.5 %all-gather = bf16[8,1,128]{2,1,0:T(2,128)(2,1)S(1)} all-gather(bf16[1,1,128]{2,1,0:T(2,128)(2,1)} %bitcast.258), channel_id=1, replica_groups=mesh['seq'=4,'fsdp'=8] {'fsdp'}, dimensions={0}, use_global_device_ids=true | all-gather | bytes 2304 | tf_op jit(solution)/shard_map/all_gather | solution.py:84
  23.8 16.5 %all_gather.49 = bf16[2,256,512]{2,1,0:T(8,128)(2,1)S(1)} all-gather(bf16[2,32,512]{2,1,0:T(8,128)(2,1)} %param.22), channel_id=1, replica_groups=mesh['seq'=4,'fsdp'=8] {'fsdp'}, dimensions={1}, use_global_device_ids=true | all-gather | bytes 589824 | tf_op jit(solution)/shard_map/all_gather | solution.py:88
  40.3 2.6 convolution_convert_fusion.13
  44.5 17.0 %all_gather.51 = bf16[2,256,512]{2,1,0:T(8,128)(2,1)S(1)} all-gather(bf16[2,32,512]{2,1,0:T(8,128)(2,1)S(1)} %copy-done.15), channel_id=1, replica_groups=mesh['seq'=4,'fsdp'=8] {'fsdp'}, dimensions={1}, use_global_device_ids=true | all-gather | bytes 589824 | tf_op jit(solution)/shard_map/all_gather | solution.py:89
  66.5 9.1 all-gather.1
  75.7 2.9 convolution_convert_fusion.9
  80.9 44.8 %all-gather.15.cloned.1.call-done = bf16[2048,1024]{0,1:T(8,128)(2,1)} async-done(((bf16[512,1024]{0,1:T(8,128)(2,1)}), bf16[2048,1024]{0,1:T(8,128)(2,1)}) %all-gather.15.cloned.1.call-update) | async-done | bytes 4194320 | tf_op jit(solution)/shard_map/all_gather | solution.py:109
  125.7 8.5 copy.48
  134.2 46.4 %all-gather.17.cloned.1.call-done = bf16[2048,1024]{0,1:T(8,128)(2,1)} async-done(((bf16[512,1024]{0,1:T(8,128)(2,1)}), bf16[2048,1024]{0,1:T(8,128)(2,1)}) %all-gather.17.cloned.1.call-update) | async-done | bytes 4194320 | tf_op jit(solution)/shard_map/all_gather | solution.py:110
  180.6 8.5 copy.49
  189.1 78.6 %while.28 = (s32[]{:T(128)}, bf16[16,512,64]{1,2,0:T(8,128)(2,1)S(1)}, f32[16,512]{1,0:T(8,128)S(1)}, bf16[16,512,64]{2,1,0:T(8,128)(2,1)}, bf16[16,2048,64]{2,1...) while((s32[]{:T(128)}, ...), condition=%wide.region_4.5_spmd.clone, body=%wide.region_1.4_spmd.clone.sunk | while | flops 277872128 | bytes 13926513 | solution.py:135
  268.7 3.3 multiply_reduce_fusion.3
  273.2 7.7 convolution_convert_fusion.3
  280.9 52.5 %all-gather.21.cloned.1.call-done = bf16[1024,2816]{1,0:T(8,128)(2,1)} async-done(((bf16[128,2816]{1,0:T(8,128)(2,1)}), bf16[1024,2816]{1,0:T(8,128)(2,1)}) %all-gather.21.cloned.1.call-update) | async-done | bytes 5767184 | tf_op jit(solution)/shard_map/all_gather | solution.py:93
  333.4 8.6 fusion.78
  342.0 52.2 %all-gather.23.cloned.1.call-done = bf16[1024,2816]{1,0:T(8,128)(2,1)} async-done(((bf16[128,2816]{1,0:T(8,128)(2,1)}), bf16[1024,2816]{1,0:T(8,128)(2,1)}) %all-gather.23.cloned.1.call-update) | async-done | bytes 5767184 | tf_op jit(solution)/shard_map/all_gather | solution.py:94
  394.2 10.8 fusion.46
  405.0 3.2 fusion.79
  409.7 3.5 multiply_reduce_fusion.1
  420.9 187.0 %while.29 = (s32[]{:T(128)}, bf16[16,512,64]{1,2,0:T(8,128)(2,1)}, bf16[16,2048,64]{1,2,0:T(8,128)(2,1)}, bf16[16,2048,64]{1,2,0:T(8,128)(2,1)}, bf16[16,512,64]...) while((s32[]{:T(128)}, bf16[16,512,64]{1,2,0:T(8,128)(2,1)}, ...), condition=%wide.region_9.10_spmd.clone, body=%wide.region_7.9_spmd.clone.sunk | while | flops 682786304 | bytes 34628736 | solution.py:202
  423.1 2.7 multiply_reduce_fusion.5
  434.8 2.7 multiply_reduce_fusion.5
  437.9 2.5 fusion.153
  446.4 2.7 multiply_reduce_fusion.5
  449.6 2.5 fusion.153
  458.1 2.7 multiply_reduce_fusion.5
  469.7 2.7 multiply_reduce_fusion.5
  481.4 2.7 multiply_reduce_fusion.5
  484.6 2.5 fusion.153
  493.0 2.7 multiply_reduce_fusion.5
  504.7 2.7 multiply_reduce_fusion.5
  516.3 2.8 multiply_reduce_fusion.5
  519.5 2.5 fusion.153
  528.0 2.7 multiply_reduce_fusion.5
  539.7 2.7 multiply_reduce_fusion.5
  551.3 2.7 multiply_reduce_fusion.5
  563.0 2.7 multiply_reduce_fusion.5
  574.7 2.7 multiply_reduce_fusion.5
  586.4 2.7 multiply_reduce_fusion.5
  598.0 2.7 multiply_reduce_fusion.5
  601.2 2.5 fusion.153
  608.5 4.0 convolution_convert_fusion.5
  612.6 5.0 convolution_convert_fusion.4
  617.7 41.7 %reduce-scatter.11.cloned.1.call-done = bf16[512,1024]{0,1:T(8,128)(2,1)} async-done(((bf16[2048,1024]{0,1:T(8,128)(2,1)}), bf16[512,1024]{0,1:T(8,128)(2,1)}) %reduce-scatter.11.cloned.1.call-update) | async-done | bytes 1048592 | tf_op jit(solution)/shard_map/reduce_scatter | solution.py:208
  659.4 2.6 convolution_convert_fusion.12
  662.2 53.0 %reduce-scatter.13.cloned.1.call-done = bf16[512,1024]{0,1:T(8,128)(2,1)} async-done(((bf16[2048,1024]{0,1:T(8,128)(2,1)}), bf16[512,1024]{0,1:T(8,128)(2,1)}) %reduce-scatter.13.cloned.1.call-update) | async-done | bytes 1048592 | tf_op jit(solution)/shard_map/reduce_scatter | solution.py:211
  715.2 2.6 convolution_convert_fusion.11
  723.1 8.0 convolution_convert_fusion.2
  731.3 7.9 convolution_convert_fusion.1
  739.3 7.8 convolution_convert_fusion
  747.2 6.6 reduce-scatter.15.cloned.1.call-done
  753.8 36.6 %reduce-scatter.23.cloned.1.call-done = bf16[128,1024]{1,0:T(8,128)(2,1)} async-done(((bf16[1024,1024]{1,0:T(8,128)(2,1)}), bf16[128,1024]{1,0:T(8,128)(2,1)}) %reduce-scatter.23.cloned.1.call-update) | async-done | bytes 262160 | tf_op jit(solution)/shard_map/reduce_scatter | solution.py:237
  790.5 32.5 %reduce-scatter.19.cloned.1.call-done = bf16[2,32,512]{2,1,0:T(8,128)(2,1)} async-done(((bf16[2,256,512]{2,1,0:T(8,128)(2,1)}), bf16[2,32,512]{2,1,0:T(8,128)(2,1)}) %reduce-scatter.19.cloned.1.call-update) | async-done | bytes 65552 | tf_op jit(solution)/shard_map/reduce_scatter | solution.py:240
  823.0 31.4 %reduce-scatter.21.cloned.1.call-done = bf16[2,32,512]{2,1,0:T(8,128)(2,1)} async-done(((bf16[2,256,512]{2,1,0:T(8,128)(2,1)}), bf16[2,32,512]{2,1,0:T(8,128)(2,1)}) %reduce-scatter.21.cloned.1.call-update) | async-done | bytes 65552 | tf_op jit(solution)/shard_map/reduce_scatter | solution.py:243
  854.3 33.2 %reduce-scatter.17.cloned.1.call-done = bf16[128,512]{1,0:T(8,128)(2,1)} async-done(((bf16[1024,512]{1,0:T(8,128)(2,1)}), bf16[128,512]{1,0:T(8,128)(2,1)}) %reduce-scatter.17.cloned.1.call-update) | async-done | bytes 131088 | tf_op jit(solution)/shard_map/reduce_scatter | solution.py:234
  887.6 65.3 %reduce-scatter.25.cloned.1.call-done = bf16[128,2816]{1,0:T(8,128)(2,1)} async-done(((bf16[1024,2816]{1,0:T(8,128)(2,1)}), bf16[128,2816]{1,0:T(8,128)(2,1)}) %reduce-scatter.25.cloned.1.call-update) | async-done | bytes 720912 | tf_op jit(solution)/shard_map/reduce_scatter | solution.py:251
  952.9 65.4 %reduce-scatter.27.cloned.1.call-done = bf16[128,2816]{1,0:T(8,128)(2,1)} async-done(((bf16[1024,2816]{1,0:T(8,128)(2,1)}), bf16[128,2816]{1,0:T(8,128)(2,1)}) %reduce-scatter.27.cloned.1.call-update) | async-done | bytes 720912 | tf_op jit(solution)/shard_map/reduce_scatter | solution.py:254
  1018.3 65.4 %reduce-scatter.29.cloned.1.call-done = bf16[352,1024]{1,0:T(8,128)(2,1)} async-done(((bf16[2816,1024]{1,0:T(8,128)(2,1)}), bf16[352,1024]{1,0:T(8,128)(2,1)}) %reduce-scatter.29.cloned.1.call-update) | async-done | bytes 720912 | tf_op jit(solution)/shard_map/reduce_scatter | solution.py:257
  1085.0 3.4 fusion.80
  1088.4 6.9 fusion.66
  1096.5 13.6 %all-reduce.2 = (bf16[1024]{0:T(1024)(128)(2,1)S(1)}, bf16[1024]{0:T(1024)(128)(2,1)S(1)}) all-reduce(bf16[1024]{0:T(1024)(128)(2,1)S(1)} %get-tuple-element.195, bf16[1024]{0:T(1024)(128)(2,1)S(1)} %get-tuple-element.193), channel_id=4, replica_groups=mesh['seq'=4,'fsdp'=8] {'fsdp'}, use_global_device_ids=true, to_apply=%region_14.15.clone | all-reduce | flops 2048 | bytes 8192
  1110.3 10.1 all-reduce.3
  1121.4 3.5 fusion.61
  1124.9 46.4 %all-reduce.7.cloned.1.call-done = (bf16[128,1024]{1,0:T(8,128)(2,1)}, bf16[128,512]{1,0:T(8,128)(2,1)}, bf16[2,32,512]{2,1,0:T(8,128)(2,1)}, bf16[2,32,512]{2,1...) async-done(((bf16[128,1024]{1,0:T(8,128)(2,1)}, bf16[128,512]{1,0:T(8,128)(2,1)}, ...) | async-done | bytes 2949136 | tf_op jit(solution)/shard_map/psum | solution.py:263
  (299 shorter events, 253.7 us)
Async XLA Ops:
  7.2 33.1 %all-gather.13.cloned.1.call-start = ((), (), s32[]{:S(2)}) async-start(), calls=%async_computation.11 | async-start | bytes 1179648 | tf_op jit(solution)/shard_map/all_gather | solution.py:86
  7.9 67.7 %all-gather.11.cloned.1.call-start = ((), (), s32[]{:S(2)}) async-start(), calls=%async_computation.10 | async-start | bytes 2359296 | tf_op jit(solution)/shard_map/all_gather | solution.py:85
  8.7 117.0 %all-gather.15.cloned.1.call-start = ((), (), s32[]{:S(2)}) async-start(), calls=%async_computation.12 | async-start | bytes 5242880 | tf_op jit(solution)/shard_map/all_gather | solution.py:109
  40.3 4.1 copy-start.3
  40.3 4.1 copy-start.15
  42.9 20.8 %copy-start.2 = (bf16[512,512]{0,1:T(8,128)(2,1)}, bf16[512,512]{0,1:T(8,128)(2,1)S(1)}, u32[]{:S(2)}) copy-start(bf16[512,512]{0,1:T(8,128)(2,1)S(1)} %convolution_convert_fusion.13) | copy-start | bytes 1572868
  44.4 136.2 %all-gather.17.cloned.1.call-start = ((), (), s32[]{:S(2)}) async-start(), calls=%async_computation.13 | async-start | bytes 5242880 | tf_op jit(solution)/shard_map/all_gather | solution.py:110
  61.5 0.8 copy-start.4
  62.3 4.3 copy-start.16
  62.3 13.3 %copy-start.17 = (s32[1,2048]{1,0:T(1,128)S(1)}, s32[1,2048]{1,0:T(1,128)}, u32[]{:S(2)}) copy-start(s32[1,2048]{1,0:T(1,128)} %param.18) | copy-start | bytes 24580
  62.3 13.4 %copy-start = (bf16[1,512,1024]{2,1,0:T(8,128)(2,1)S(1)}, bf16[1,512,1024]{2,1,0:T(8,128)(2,1)}, u32[]{:S(2)}) copy-start(bf16[1,512,1024]{2,1,0:T(8,128)(2,1)} %param.17) | copy-start | bytes 3145732
  63.8 204.0 %all-gather.19.cloned.1.call-start = ((), (), s32[]{:S(2)}) async-start(), calls=%async_computation.14 | async-start | bytes 2359296 | tf_op jit(solution)/shard_map/all_gather | solution.py:87
  64.4 208.9 %all-gather.25.cloned.1.call-start = ((), (), s32[]{:S(2)}) async-start(), calls=%async_computation.17 | async-start | bytes 6488064 | tf_op jit(solution)/shard_map/all_gather | solution.py:95
  64.9 268.5 %all-gather.21.cloned.1.call-start = ((), (), s32[]{:S(2)}) async-start(), calls=%async_computation.15 | async-start | bytes 6488064 | tf_op jit(solution)/shard_map/all_gather | solution.py:93
  65.7 328.5 %all-gather.23.cloned.1.call-start = ((), (), s32[]{:S(2)}) async-start(), calls=%async_computation.16 | async-start | bytes 6488064 | tf_op jit(solution)/shard_map/all_gather | solution.py:94
  66.4 593.0 %reduce-scatter.11.cloned.1.call-start = ((), (), s32[]{:S(2)}) async-start(), calls=%async_computation.18 | async-start | bytes 5242880 | tf_op jit(solution)/shard_map/reduce_scatter | solution.py:208
  267.7 1.0 copy-start.7
  394.2 10.8 copy-start.18
  405.0 3.2 copy-start.23
  405.0 3.2 copy-start.21
  405.0 4.7 copy-start.19
  409.7 3.5 copy-start.12
  413.2 2.0 copy-start.8
  413.8 1.4 copy-start.1
  607.9 107.3 %reduce-scatter.13.cloned.1.call-start = ((), (), s32[]{:S(2)}) async-start(), calls=%async_computation.19 | async-start | bytes 5242880 | tf_op jit(solution)/shard_map/reduce_scatter | solution.py:211
  608.5 145.3 %reduce-scatter.15.cloned.1.call-start = ((), (), s32[]{:S(2)}) async-start(), calls=%async_computation.20 | async-start | bytes 2359296 | tf_op jit(solution)/shard_map/reduce_scatter | solution.py:231
  612.6 177.9 %reduce-scatter.23.cloned.1.call-start = ((), (), s32[]{:S(2)}) async-start(), calls=%async_computation.24 | async-start | bytes 2359296 | tf_op jit(solution)/shard_map/reduce_scatter | solution.py:237
  617.7 205.3 %reduce-scatter.19.cloned.1.call-start = ((), (), s32[]{:S(2)}) async-start(), calls=%async_computation.22 | async-start | bytes 589824 | tf_op jit(solution)/shard_map/reduce_scatter | solution.py:240
  662.1 192.2 %reduce-scatter.21.cloned.1.call-start = ((), (), s32[]{:S(2)}) async-start(), calls=%async_computation.23 | async-start | bytes 589824 | tf_op jit(solution)/shard_map/reduce_scatter | solution.py:243
  717.8 169.7 %reduce-scatter.17.cloned.1.call-start = ((), (), s32[]{:S(2)}) async-start(), calls=%async_computation.21 | async-start | bytes 1179648 | tf_op jit(solution)/shard_map/reduce_scatter | solution.py:234
  717.9 2.0 copy-start.5
  717.9 2.0 copy-start.6
  720.3 0.8 copy-start.9
  723.0 229.9 %reduce-scatter.25.cloned.1.call-start = ((), (), s32[]{:S(2)}) async-start(), calls=%async_computation.25 | async-start | bytes 6488064 | tf_op jit(solution)/shard_map/reduce_scatter | solution.py:251
  731.1 287.2 %reduce-scatter.27.cloned.1.call-start = ((), (), s32[]{:S(2)}) async-start(), calls=%async_computation.26 | async-start | bytes 6488064 | tf_op jit(solution)/shard_map/reduce_scatter | solution.py:254
  739.3 344.5 %reduce-scatter.29.cloned.1.call-start = ((), (), s32[]{:S(2)}) async-start(), calls=%async_computation.27 | async-start | bytes 6488064 | tf_op jit(solution)/shard_map/reduce_scatter | solution.py:257
  747.2 336.6 %copy-start.20 = (u32[32]{0:T(128)S(1)}, u32[32]{0:T(128)}, u32[]{:S(2)}) copy-start(u32[32]{0:T(128)} %constant.77) | copy-start | bytes 388
  747.2 424.1 %all-reduce.7.cloned.1.call-start = ((), (), s32[]{:S(2)}) async-start(), calls=%async_computation.28 | async-start | bytes 5898240 | tf_op jit(solution)/shard_map/psum | solution.py:263
  1085.0 3.4 copy-start.22
  1088.4 6.9 copy-start.10
  1088.4 6.9 copy-start.11
  1171.3 10.7 copy-start.14
  1173.2 10.0 copy-start.13
Sparse Core Ops, SparseCore 0:
  9.6 27.6 all-gather.12
  38.9 32.1 all-gather.10
  73.4 52.2 all-gather.14
  128.0 52.5 all-gather.16
  182.0 29.0 all-gather.18
  212.7 59.9 all-gather.24
  274.2 59.0 all-gather.20
  335.0 59.0 all-gather.22
  608.0 51.3 reduce-scatter.10
  662.5 52.6 reduce-scatter.12
  718.0 35.7 reduce-scatter.14
  756.0 34.4 reduce-scatter.22
  793.3 29.6 reduce-scatter.18
  825.2 29.1 reduce-scatter.20
  857.0 30.4 reduce-scatter.16
  889.7 63.1 reduce-scatter.24
  955.0 63.2 reduce-scatter.26
  1020.5 63.2 reduce-scatter.28
  1087.6 83.6 all-reduce.6
where the time goes:
time: 1200 us; the launch traced here: 1190 us
  waiting for transfers between devices  678 us (56%)
  matrix products  346 us (29%)
  blocking collectives  79.9 us (7%)
  other arithmetic  39.3 us (3%)
  local copies, waits for them, and re-layouts  30.2 us (3%)
  between operations  15.2 us (1%)
    dot_general x32, matrix products, masked_scores(): jnp.einsum('qd,kd->qk', query_head, key_head, preferred_element_type=jnp....  75.7 us
    reduce_scatter x1, waiting for transfers between devices, local(): lax.psum_scatter(grad_down.astype(jnp.bfloat16), 'fsdp', scatter_dimensio...  65.4 us
    reduce_scatter x1, waiting for transfers between devices, local(): lax.psum_scatter(grad_upper.astype(jnp.bfloat16), 'fsdp', scatter_dimensi...  65.4 us
    reduce_scatter x1, waiting for transfers between devices, local(): lax.psum_scatter(grad_gate.astype(jnp.bfloat16), 'fsdp', scatter_dimensio...  65.3 us
    reduce_scatter x1, waiting for transfers between devices, local(): lax.psum_scatter(value_terms.astype(jnp.bfloat16), 'seq', scatter_dimensi...  53 us
    all_gather x1, waiting for transfers between devices, local(): lax.all_gather(w_gate, 'fsdp', axis=0, tiled=True)  52.5 us
    all_gather x1, waiting for transfers between devices, local(): lax.all_gather(w_up, 'fsdp', axis=0, tiled=True)  52.2 us
    psum x1, waiting for transfers between devices, local(): lax.psum(part_query.astype(jnp.bfloat16), 'seq').astype(jnp.float32)  46.4 us
  transfers between devices with their start and end apart: 19, of which 15 were waited for; matrix products, arithmetic and copies ran while one was open for 16% of the time, Pallas kernels for 0%

commit v1 on v0

--- a/solution.py
+++ b/solution.py
@@ -1,6 +1,8 @@
 import jax
 import jax.numpy as jnp
 from jax import lax
+from jax.experimental import pallas as pl
+from jax.experimental.pallas import tpu as pltpu
 from jax.sharding import PartitionSpec as P
 
 HEADS = 16
@@ -286,6 +288,905 @@
     )
 
 
+MESH = pl.DeviceIdType.MESH
+NEG = -1e30
+WIDE = 60 * 2**20
+BF = jnp.bfloat16
+F32 = jnp.float32
+
+
+def dot(a, b):
+    return jnp.dot(a, b, preferred_element_type=F32)
+
+
+def dot_t(a, b):
+    return lax.dot_general(a, b, (((1,), (1,)), ((), ())), preferred_element_type=F32)
+
+
+def dot_l(a, b):
+    return lax.dot_general(a, b, (((0,), (0,)), ((), ())), preferred_element_type=F32)
+
+
+class Place:
+    def __init__(self):
+        s, f = lax.axis_index("seq"), lax.axis_index("fsdp")
+        self.s, self.f = s, f
+        self.z, self.c = lax.div(f, 2), lax.rem(f, 2)
+        self.xs = s + 1 - 2 * lax.rem(s, 2)
+        self.ys = s + 2 - 4 * lax.div(s, 2)
+        self.ds = 3 - s
+        self.sib = f + 1 - 2 * self.c
+        self.half = lax.div(self.z, 2)
+        self.inner = lax.rem(lax.div(self.z + 1, 2), 2)
+
+    def greet(self, line=True, sibling=True):
+        bar = pltpu.get_barrier_semaphore()
+
+        def hail(seq, fsdp):
+            pl.semaphore_signal(bar, inc=1, device_id=(seq, fsdp), device_id_type=MESH)
+
+        hail(self.xs, self.f)
+        hail(self.ys, self.f)
+        count = 2
+        if sibling:
+            hail(self.s, self.sib)
+            count = count + 1
+        if line:
+            pl.when(self.z < 3)(lambda: hail(self.s, self.f + 2))
+            pl.when(self.z > 0)(lambda: hail(self.s, self.f - 2))
+            count = count + 1 + self.inner
+        pl.semaphore_wait(bar, count)
+
+
+class Wire:
+    def __init__(self, sends, recvs, tensor):
+        self.sends, self.recvs, self.tensor = sends, recvs, tensor
+        self.sent = []
+
+    def copy(self, kind, src, dst, dev):
+        return pltpu.make_async_remote_copy(
+            src_ref=src,
+            dst_ref=dst,
+            send_sem=self.sends.at[self.tensor, kind],
+            recv_sem=self.recvs.at[self.tensor, kind],
+            device_id=dev,
+            device_id_type=MESH,
+        )
+
+    def send(self, kind, src, dst, dev, cond=None):
+        self.copy(kind, src, dst, dev).start()
+        self.sent.append((kind, src, dst, dev, cond))
+
+    def recv(self, kind, landing, dev):
+        self.copy(kind, landing, landing, dev).wait_recv()
+
+    def drain(self):
+        for kind, src, dst, dev, cond in self.sent:
+            if cond is None:
+                self.copy(kind, src, dst, dev).wait_send()
+            else:
+                pl.when(cond)(lambda k=kind, a=src, b=dst, d=dev: self.copy(k, a, b, d).wait_send())
+        self.sent = []
+
+
+class Gather:
+    KINDS = 37
+
+    def __init__(self, here, shards, fulls, cuts, sends, recvs, locals_):
+        self.here, self.shards, self.fulls, self.cuts, self.locals = here, shards, fulls, cuts, locals_
+        self.wires = [Wire(sends, recvs, t) for t in range(len(shards))]
+        self.each = list(zip(range(len(shards)), self.wires, shards, fulls, cuts))
+
+    def slot(self, way, d):
+        h = self.here
+        j = way * 3 + d - 1
+        if way == 0:
+            return j, h.z >= d, h.f - 2 * d, jnp.logical_and(h.z >= d, h.z < 3), h.f + 2
+        return j, h.z + d <= 3, h.f + 2 * d, jnp.logical_and(h.z + d <= 3, h.z > 0), h.f - 2
+
+    def own(self, t, shard, full):
+        return pltpu.make_async_copy(shard, full.at[self.here.f], self.locals.at[t])
+
+    def start(self):
+        h = self.here
+        up, down = h.z < 3, h.z > 0
+        above, below = (h.s, h.f + 2), (h.s, h.f - 2)
+        for t, w, shard, full, cut in self.each:
+            mine, there = shard.at[h.s], full.at[h.f, h.s]
+            pl.when(up)(lambda: w.send(0, mine, there, above, up))
+            pl.when(down)(lambda: w.send(3, mine, there, below, down))
+        for t, w, shard, full, cut in self.each:
+            w.send(36, shard, full.at[h.f], (h.s, h.sib))
+            self.own(t, shard, full).start()
+
+    def line(self, way, d, which=None):
+        h = self.here
+        j, act, fp, more, onward = self.slot(way, d)
+        for t, w, shard, full, cut in self.each if which is None else [self.each[i] for i in which]:
+            piece = full.at[fp, h.s]
+
+            @pl.when(act)
+            def _():
+                w.recv(j, piece, (h.s, h.f))
+                if d < 3:
+                    pl.when(more)(lambda: w.send(j + 1, piece, piece, (h.s, onward), more))
+                w.send(6 + j, piece, piece, (h.xs, h.f), act)
+                w.send(12 + j, piece, piece, (h.ys, h.f), act)
+
+    def turn(self, way, d, which=None):
+        h = self.here
+        j, act, fp, more, onward = self.slot(way, d)
+        for t, w, shard, full, cut in self.each if which is None else [self.each[i] for i in which]:
+            q = full.shape[2]
+            part = full.at[fp, h.xs, pl.ds(0, cut)]
+            rest = full.at[fp, h.ys, pl.ds(cut, q - cut)] if cut < q else None
+
+            @pl.when(act)
+            def _():
+                w.recv(6 + j, full.at[fp, h.xs], (h.xs, h.f))
+                w.send(18 + j, part, part, (h.ys, h.f), act)
+                w.recv(12 + j, full.at[fp, h.ys], (h.ys, h.f))
+                if cut < q:
+                    w.send(24 + j, rest, rest, (h.xs, h.f), act)
+
+    def cross(self, way, d, which=None):
+        h = self.here
+        j, act, fp, more, onward = self.slot(way, d)
+        for t, w, shard, full, cut in self.each if which is None else [self.each[i] for i in which]:
+            q = full.shape[2]
+            shard = full.at[fp]
+
+            @pl.when(act)
+            def _():
+                w.recv(18 + j, full.at[fp, h.ds, pl.ds(0, cut)], (h.ys, h.f))
+                if cut < q:
+                    w.recv(24 + j, full.at[fp, h.ds, pl.ds(cut, q - cut)], (h.xs, h.f))
+                w.send(30 + j, shard, shard, (h.s, h.sib), act)
+
+    def finish(self):
+        h = self.here
+        for t, w, shard, full, cut in self.each:
+            w.recv(36, full.at[h.sib], (h.s, h.sib))
+            for way in range(2):
+                for d in (1, 2, 3):
+                    j, act, fp, more, onward = self.slot(way, d)
+                    theirs = fp + 1 - 2 * h.c
+                    pl.when(act)(lambda: w.recv(30 + j, full.at[theirs], (h.s, h.sib)))
+            self.own(t, shard, full).wait()
+            w.drain()
+
+    def program(self):
+        steps = [self.start]
+
+        def at(what, d):
+            return [lambda way=way: what(way, d) for way in range(2)]
+
+        steps += at(self.line, 1) + at(self.turn, 1) + at(self.line, 2) + at(self.cross, 1)
+        steps += at(self.turn, 2) + at(self.line, 3) + at(self.cross, 2) + at(self.turn, 3)
+        steps += at(self.cross, 3) + [self.finish]
+        return steps
+
+
+def gather_call(shards, cuts, collective_id, name):
+    count = len(shards)
+
+    def kernel(*refs):
+        ins, outs = refs[:count], refs[count : 2 * count]
+        sends, recvs, locals_ = refs[2 * count :]
+        here = Place()
+        here.greet()
+        for step in Gather(here, ins, outs, cuts, sends, recvs, locals_).program():
+            step()
+
+    shapes = [jax.ShapeDtypeStruct((8,) + a.shape, a.dtype) for a in shards]
+    return pl.pallas_call(
+        kernel,
+        name=name,
+        out_shape=shapes,
+        in_specs=[pl.BlockSpec(memory_space=pl.ANY)] * count,
+        out_specs=[pl.BlockSpec(memory_space=pl.ANY)] * count,
+        scratch_shapes=[
+            pltpu.SemaphoreType.DMA((count, Gather.KINDS)),
+            pltpu.SemaphoreType.DMA((count, Gather.KINDS)),
+            pltpu.SemaphoreType.DMA((count,)),
+        ],
+        compiler_params=pltpu.CompilerParams(
+            collective_id=collective_id, has_side_effects=True, vmem_limit_bytes=WIDE
+        ),
+    )(*shards)
+
+
+def rows_of(q):
+    return 16 if q % 16 == 0 else q
+
+
+def add_into(target, others):
+    q = target.shape[0]
+    step = rows_of(q)
+
+    def body(r):
+        total = target[r, :].astype(F32)
+        for other in others:
+            total = total + other[r, :].astype(F32)
+        target[r, :] = total.astype(target.dtype)
+
+    if step == q:
+        body(slice(0, q))
+    else:
+
+        @pl.loop(0, q // step)
+        def _(k):
+            body(pl.ds(pl.multiple_of(k * step, step), step))
+
+
+class Reduce:
+    KINDS = 32
+
+    @staticmethod
+    def scratch(shapes, cuts):
+        out = []
+        for (q, cols), cut in zip(shapes, cuts):
+            out += [
+                pltpu.VMEM((4, 4, q, cols), BF),
+                pltpu.VMEM((4, 4, q, cols), BF),
+                pltpu.VMEM((4, cut, cols), BF),
+                pltpu.VMEM((4, max(q - cut, 8), cols), BF),
+                pltpu.VMEM((4, q, cols), BF),
+                pltpu.VMEM((4, q, cols), BF),
+                pltpu.VMEM((2, 4, q, cols), BF),
+            ]
+        n = len(shapes)
+        return out + [
+            pltpu.SemaphoreType.DMA((n, Reduce.KINDS)),
+            pltpu.SemaphoreType.DMA((n, Reduce.KINDS)),
+            pltpu.SemaphoreType.DMA((n, 5)),
+        ]
+
+    def __init__(self, here, parts, outs, cuts, scratch):
+        n = len(parts)
+        sends, recvs, self.locals = scratch[7 * n :]
+        self.here = here
+        self.each = [
+            (t, Wire(sends, recvs, t), parts[t], outs[t], cuts[t]) + tuple(scratch[7 * t : 7 * t + 7])
+            for t in range(n)
+        ]
+
+    def target(self, i):
+        h = self.here
+        if i < 2:
+            return 3 - 3 * h.half + i * (2 * h.half - 1)
+        return 1 - h.z + 4 * h.half if i == 2 else h.z
+
+    def load(self, t, part, acc, i):
+        return pltpu.make_async_copy(
+            part.at[2 * self.target(i) + self.here.c], acc.at[i], self.locals.at[t, i]
+        )
+
+    def start(self):
+        h = self.here
+        for i in range(4):
+            for t, w, part, out, cut, acc, sib, da, db, xb, yb, zb in self.each:
+                w.send(i, part.at[2 * self.target(i) + 1 - h.c], sib.at[i], (h.s, h.sib))
+                self.load(t, part, acc, i).start()
+
+    def pair(self, i):
+        h = self.here
+        for t, w, part, out, cut, acc, sib, da, db, xb, yb, zb in self.each:
+            self.load(t, part, acc, i).wait()
+            w.recv(i, sib.at[i], (h.s, h.sib))
+            for p in range(4):
+                add_into(acc.at[i, p], [sib.at[i, p]])
+            q = acc.shape[2]
+            w.send(4 + i, acc.at[i, h.ds, pl.ds(0, cut)], da.at[i], (h.ys, h.f))
+            if cut < q:
+                w.send(8 + i, acc.at[i, h.ds, pl.ds(cut, q - cut)], db.at[i], (h.xs, h.f))
+
+    def turn(self, i):
+        h = self.here
+        for t, w, part, out, cut, acc, sib, da, db, xb, yb, zb in self.each:
+            q = acc.shape[2]
+            w.recv(4 + i, da.at[i], (h.ys, h.f))
+            add_into(acc.at[i, h.xs, pl.ds(0, cut)], [da.at[i]])
+            if cut < q:
+                w.recv(8 + i, db.at[i], (h.xs, h.f))
+                add_into(acc.at[i, h.ys, pl.ds(cut, q - cut)], [db.at[i]])
+            w.send(12 + i, acc.at[i, h.xs], xb.at[i], (h.xs, h.f))
+            w.send(16 + i, acc.at[i, h.ys], yb.at[i], (h.ys, h.f))
+
+    def line(self, i):
+        h = self.here
+        zp = self.target(i)
+        for t, w, part, out, cut, acc, sib, da, db, xb, yb, zb in self.each:
+            mine = acc.at[i, h.s]
+            w.recv(12 + i, xb.at[i], (h.xs, h.f))
+            w.recv(16 + i, yb.at[i], (h.ys, h.f))
+            add_into(mine, [xb.at[i], yb.at[i]])
+            if i < 3:
+                way = h.half if i < 2 else lax.rem(h.half + h.inner, 2)
+
+                @pl.when(h.inner == 1)
+                def _():
+                    w.recv(20 + way * 4 + zp, zb.at[way, zp], (h.s, h.f))
+                    add_into(mine, [zb.at[way, zp]])
+
+                w.send(20 + way * 4 + zp, mine, zb.at[way, zp], (h.s, h.f + 2 - 4 * way))
+            else:
+
+                @pl.when(h.z > 0)
+                def _():
+                    w.recv(20 + zp, zb.at[0, zp], (h.s, h.f))
+                    add_into(mine, [zb.at[0, zp]])
+
+                @pl.when(h.z < 3)
+                def _():
+                    w.recv(24 + zp, zb.at[1, zp], (h.s, h.f))
+                    add_into(mine, [zb.at[1, zp]])
+
+                w.send(28, mine, out.at[h.s], (h.xs, h.f))
+                w.send(29, mine, out.at[h.s], (h.ys, h.f))
+                pltpu.make_async_copy(mine, out.at[h.s], self.locals.at[t, 4]).start()
+
+    def share(self):
+        h = self.here
+        for t, w, part, out, cut, acc, sib, da, db, xb, yb, zb in self.each:
+            q = acc.shape[2]
+            w.recv(28, out.at[h.xs], (h.xs, h.f))
+            piece = out.at[h.xs, pl.ds(0, cut)]
+            w.send(30, piece, piece, (h.ys, h.f))
+            w.recv(29, out.at[h.ys], (h.ys, h.f))
+            if cut < q:
+                piece = out.at[h.ys, pl.ds(cut, q - cut)]
+                w.send(31, piece, piece, (h.xs, h.f))
+
+    def finish(self):
+        h = self.here
+        for t, w, part, out, cut, acc, sib, da, db, xb, yb, zb in self.each:
+            q = acc.shape[2]
+            w.recv(30, out.at[h.ds, pl.ds(0, cut)], (h.ys, h.f))
+            if cut < q:
+                w.recv(31, out.at[h.ds, pl.ds(cut, q - cut)], (h.xs, h.f))
+            pltpu.make_async_copy(acc.at[3, h.s], out.at[h.s], self.locals.at[t, 4]).wait()
+            w.drain()
+
+    def program(self):
+        def at(what, i):
+            return lambda: what(i)
+
+        return [
+            self.start,
+            at(self.pair, 0),
+            at(self.pair, 1),
+            at(self.turn, 0),
+            at(self.pair, 2),
+            at(self.line, 0),
+            at(self.turn, 1),
+            at(self.pair, 3),
+            at(self.line, 1),
+            at(self.turn, 2),
+            at(self.line, 2),
+            at(self.turn, 3),
+            at(self.line, 3),
+            self.share,
+            self.finish,
+        ]
+
+
+def reduce_call(parts, cuts, collective_id, name):
+    count = len(parts)
+
+    def kernel(*refs):
+        ins, outs, scratch = refs[:count], refs[count : 2 * count], refs[2 * count :]
+        here = Place()
+        here.greet()
+        for step in Reduce(here, ins, outs, cuts, scratch).program():
+            step()
+
+    return pl.pallas_call(
+        kernel,
+        name=name,
+        out_shape=[jax.ShapeDtypeStruct(a.shape[1:], a.dtype) for a in parts],
+        in_specs=[pl.BlockSpec(memory_space=pl.ANY)] * count,
+        out_specs=[pl.BlockSpec(memory_space=pl.ANY)] * count,
+        scratch_shapes=Reduce.scratch([a.shape[2:] for a in parts], cuts),
+        compiler_params=pltpu.CompilerParams(
+            collective_id=collective_id, has_side_effects=True, vmem_limit_bytes=WIDE
+        ),
+    )(*parts)
+
+
+def gain_row(block, which):
+    rows = [block[32 * f + which : 32 * f + which + 1, :] for f in range(8)]
+    return jnp.concatenate(rows, axis=1).astype(F32)
+
+
+def vmem():
+    return pl.BlockSpec(memory_space=pltpu.VMEM)
+
+
+def anywhere():
+    return pl.BlockSpec(memory_space=pl.ANY)
+
+
+def project_kernel(tok, ql, gains, q_out, lat_all, lat, sends, recvs, locals_):
+    here = Place()
+    here.greet(line=False, sibling=False)
+    s, xs, ys, ds, f = here.s, here.xs, here.ys, here.ds, here.f
+    x = tok[...].astype(F32)
+    normed, _ = normalize(x)
+    h1 = (normed * gain_row(gains, 0)).astype(BF)
+    half = lat.shape[0] // 2
+    lat[...] = dot(h1, ql[:, 1024:]).astype(BF)
+    w = Wire(sends, recvs, 0)
+    w.send(0, lat, lat_all.at[s], (xs, f))
+    w.send(1, lat, lat_all.at[s], (ys, f))
+    own = pltpu.make_async_copy(lat, lat_all.at[s], locals_.at[0])
+    own.start()
+    q_out[...] = dot(h1, ql[:, :1024]).astype(BF)
+    w.recv(0, lat_all.at[xs], (xs, f))
+    top = lat_all.at[xs, pl.ds(0, half)]
+    w.send(2, top, top, (ys, f))
+    w.recv(1, lat_all.at[ys], (ys, f))
+    low = lat_all.at[ys, pl.ds(half, half)]
+    w.send(3, low, low, (xs, f))
+    w.recv(2, lat_all.at[ds, pl.ds(0, half)], (ys, f))
+    w.recv(3, lat_all.at[ds, pl.ds(half, half)], (xs, f))
+    own.wait()
+    w.drain()
+
+
+def project(tok, ql, u_full, collective_id):
+    count = tok.shape[0]
+    return pl.pallas_call(
+        project_kernel,
+        name="project",
+        grid=(1,),
+        out_shape=[
+            jax.ShapeDtypeStruct((count, 1024), BF),
+            jax.ShapeDtypeStruct((4, count, 512), BF),
+        ],
+        in_specs=[
+            pl.BlockSpec((count, 1024), lambda i: (0, 0)),
+            pl.BlockSpec((1024, 1536), lambda i: (0, 0)),
+            pl.BlockSpec((256, 128), lambda i: (0, 16)),
+        ],
+        out_specs=[pl.BlockSpec((count, 1024), lambda i: (0, 0)), anywhere()],
+        scratch_shapes=[
+            pltpu.VMEM((count, 512), BF),
+            pltpu.SemaphoreType.DMA((1, 4)),
+            pltpu.SemaphoreType.DMA((1, 4)),
+            pltpu.SemaphoreType.DMA((1,)),
+        ],
+        compiler_params=pltpu.CompilerParams(
+            collective_id=collective_id, has_side_effects=True, vmem_limit_bytes=WIDE
+        ),
+    )(tok, ql, u_full)
+
+
+def attend_kernel(q_ref, lat_ref, uk_ref, uv_ref, lim_ref, o_ref, lse_ref, k_ref, v_ref):
+    k_ref[...] = dot(lat_ref[...], uk_ref[...]).astype(BF)
+    v_ref[...] = dot(lat_ref[...], uv_ref[...]).astype(BF)
+    outs = []
+    for h in range(2):
+        cs = slice(64 * h, 64 * h + 64)
+        q = q_ref[:, cs] * jnp.asarray(0.125, BF)
+        scores = dot_t(k_ref[:, cs], q)
+        allowed = lax.broadcasted_iota(jnp.int32, scores.shape, 0) < lim_ref[...]
+        scores = jnp.where(allowed, scores, NEG)
+        peak = jnp.max(scores, axis=0, keepdims=True)
+        shifted = jnp.exp(scores - peak)
+        total = jnp.sum(shifted, axis=0, keepdims=True)
+        outs.append(dot_l(v_ref[:, cs], shifted.astype(BF)) / total)
+        lse_ref[0, h : h + 1, :] = peak + jnp.log(total)
+    o_ref[...] = jnp.concatenate(outs, axis=0).T.astype(BF)
+
+
+def attend(q, lat_full, u_full, limits):
+    count, keys = q.shape[0], lat_full.shape[0]
+    return pl.pallas_call(
+        attend_kernel,
+        name="attend",
+        grid=(8,),
+        in_specs=[
+            pl.BlockSpec((count, 128), lambda i: (0, i)),
+            pl.BlockSpec((keys, 256), lambda i: (0, i // 4)),
+            pl.BlockSpec((256, 128), lambda i: (0, i)),
+            pl.BlockSpec((256, 128), lambda i: (0, 8 + i)),
+            pl.BlockSpec((1, count), lambda i: (0, 0)),
+        ],
+        out_specs=[
+            pl.BlockSpec((count, 128), lambda i: (0, i)),
+            pl.BlockSpec((1, 2, count), lambda i: (i, 0, 0)),
+            pl.BlockSpec((keys, 128), lambda i: (0, i)),
+            pl.BlockSpec((keys, 128), lambda i: (0, i)),
+        ],
+        out_shape=[
+            jax.ShapeDtypeStruct((count, 1024), BF),
+            jax.ShapeDtypeStruct((8, 2, count), F32),
+            jax.ShapeDtypeStruct((keys, 1024), BF),
+            jax.ShapeDtypeStruct((keys, 1024), BF),
+        ],
+        compiler_params=pltpu.CompilerParams(vmem_limit_bytes=WIDE),
+    )(q, lat_full, u_full, u_full, limits)
+
+
+FF_TILES = ((0, 768), (768, 768), (1536, 640), (2176, 640))
+
+
+def feed_kernel(
+    tok, cot, mixed, wo, gains, gu, dn,
+    out, d_resid, d_heads, g_wo, g_gain, g_gu, g_dn,
+    wg, wu, wd, gg, gup, gd, h2_ref, y_acc, dh_acc, in_sems, out_sems,
+):
+    ff = dn.shape[0]
+
+    def fetch(j):
+        lo, n = FF_TILES[j]
+        b = j % 2
+        return [
+            pltpu.make_async_copy(gu.at[:, pl.ds(lo, n)], wg.at[b, :, pl.ds(0, n)], in_sems.at[b, 0]),
+            pltpu.make_async_copy(gu.at[:, pl.ds(ff + lo, n)], wu.at[b, :, pl.ds(0, n)], in_sems.at[b, 1]),
+            pltpu.make_async_copy(dn.at[pl.ds(lo, n)], wd.at[b, pl.ds(0, n)], in_sems.at[b, 2]),
+        ]
+
+    def flush(j):
+        lo, n = FF_TILES[j]
+        b = j % 2
+        return [
+            pltpu.make_async_copy(gg.at[b, :, pl.ds(0, n)], g_gu.at[:, pl.ds(lo, n)], out_sems.at[b, 0]),
+            pltpu.make_async_copy(gup.at[b, :, pl.ds(0, n)], g_gu.at[:, pl.ds(ff + lo, n)], out_sems.at[b, 1]),
+            pltpu.make_async_copy(gd.at[b, pl.ds(0, n)], g_dn.at[pl.ds(lo, n)], out_sems.at[b, 2]),
+        ]
+
+    for copy in fetch(0):
+        copy.start()
+    x = tok[...].astype(F32)
+    resid = x + dot(mixed[...], wo[...])
+    normed, inverse = normalize(resid)
+    gain = gain_row(gains, 1)
+    h2_ref[...] = (normed * gain).astype(BF)
+    y_acc[...] = resid
+    for j, (lo, n) in enumerate(FF_TILES):
+        b = j % 2
+        for copy in fetch(j):
+            copy.wait()
+        if j + 1 < len(FF_TILES):
+            for copy in fetch(j + 1):
+                copy.start()
+        if j >= 2:
+            for copy in flush(j - 2):
+                copy.wait()
+        gate_w, up_w, down_w = wg[b, :, :n], wu[b, :, :n], wd[b, :n, :]
+        h2, dy = h2_ref[...], cot[...]
+        gate = dot(h2, gate_w)
+        up = dot(h2, up_w)
+        sig = jax.nn.sigmoid(gate)
+        silu = gate * sig
+        hid = (silu * up).astype(BF)
+        y_acc[...] += dot(hid, down_w)
+        gd[b, :n, :] = dot_l(hid, dy).astype(BF)
+        d_hid = dot_t(dy, down_w).astype(BF).astype(F32)
+        d_gate = (d_hid * up * sig * (1.0 + gate * (1.0 - sig))).astype(BF)
+        d_up = (d_hid * silu).astype(BF)
+        gg[b, :, :n] = dot_l(h2, d_gate).astype(BF)
+        gup[b, :, :n] = dot_l(h2, d_up).astype(BF)
+        term = dot_t(d_gate, gate_w) + dot_t(d_up, up_w)
+        if j == 0:
+            dh_acc[...] = term
+        else:
+            dh_acc[...] += term
+        for copy in flush(j):
+            copy.start()
+    out[...] = y_acc[...].astype(BF)
+    resid = tok[...].astype(F32) + dot(mixed[...], wo[...])
+    normed, inverse = normalize(resid)
+    dh = dh_acc[...]
+    g_gain[...] = jnp.sum(dh * normed, axis=0, keepdims=True)
+    back = cot[...].astype(F32) + norm_back(dh * gain, normed, inverse)
+    d_resid[...] = back
+    d_attn = back.astype(BF)
+    d_heads[...] = dot_t(d_attn, wo[...]).astype(BF)
+    g_wo[...] = dot_l(mixed[...], d_attn).astype(BF)
+    for j in (len(FF_TILES) - 2, len(FF_TILES) - 1):
+        for copy in flush(j):
+            copy.wait()
+
+
+def feed(tok, cot, mixed, wo, u_full, gu, dn):
+    count = tok.shape[0]
+    whole = lambda *shape: pl.BlockSpec(shape, lambda i: (0,) * len(shape))
+    return pl.pallas_call(
+        feed_kernel,
+        name="feed",
+        grid=(1,),
+        in_specs=[
+            vmem(), vmem(), vmem(), vmem(),
+            pl.BlockSpec((256, 128), lambda i: (0, 16)),
+            anywhere(), anywhere(),
+        ],
+        out_specs=[vmem(), vmem(), vmem(), vmem(), vmem(), anywhere(), anywhere()],
+        out_shape=[
+            jax.ShapeDtypeStruct((count, 1024), BF),
+            jax.ShapeDtypeStruct((count, 1024), F32),
+            jax.ShapeDtypeStruct((count, 1024), BF),
+            jax.ShapeDtypeStruct((1024, 1024), BF),
+            jax.ShapeDtypeStruct((1, 1024), F32),
+            jax.ShapeDtypeStruct(gu.shape, BF),
+            jax.ShapeDtypeStruct(dn.shape, BF),
+        ],
+        scratch_shapes=[
+            pltpu.VMEM((2, 1024, 768), BF),
+            pltpu.VMEM((2, 1024, 768), BF),
+            pltpu.VMEM((2, 768, 1024), BF),
+            pltpu.VMEM((2, 1024, 768), BF),
+            pltpu.VMEM((2, 1024, 768), BF),
+            pltpu.VMEM((2, 768, 1024), BF),
+            pltpu.VMEM((count, 1024), BF),
+            pltpu.VMEM((count, 1024), F32),
+            pltpu.VMEM((count, 1024), F32),
+            pltpu.SemaphoreType.DMA((2, 3)),
+            pltpu.SemaphoreType.DMA((2, 3)),
+        ],
+        compiler_params=pltpu.CompilerParams(vmem_limit_bytes=WIDE),
+    )(tok, cot, mixed, wo, u_full, gu, dn)
+
+
+KEY_TILE = 1024
+
+
+def attend_back_kernel(
+    q_ref, k_ref, v_ref, do_ref, o_ref, lse_ref, lim_ref, lat_ref, uk_ref, uv_ref,
+    dq_ref, dlat_ref, guk_ref, guv_ref, dlat_acc, dk_all, dv_all, dq_acc,
+):
+    i = pl.program_id(0)
+    keys = k_ref.shape[0]
+    deltas = []
+    for h in range(2):
+        cs = slice(64 * h, 64 * h + 64)
+        prod = do_ref[:, cs].astype(F32) * o_ref[:, cs].astype(F32)
+        deltas.append(jnp.sum(prod.T, axis=0, keepdims=True))
+    dq_acc[...] = jnp.zeros_like(dq_acc)
+
+    @pl.loop(0, keys // KEY_TILE)
+    def _(t):
+        rows = pl.ds(pl.multiple_of(t * KEY_TILE, KEY_TILE), KEY_TILE)
+        d_keys, d_values = [], []
+        for h in range(2):
+            cs = slice(64 * h, 64 * h + 64)
+            q = q_ref[:, cs] * jnp.asarray(0.125, BF)
+            d_out = do_ref[:, cs]
+            key, value = k_ref[rows, cs], v_ref[rows, cs]
+            scores = dot_t(key, q)
+            place = lax.broadcasted_iota(jnp.int32, scores.shape, 0) + t * KEY_TILE
+            probs = jnp.where(place < lim_ref[...], jnp.exp(scores - lse_ref[0, h : h + 1, :]), 0.0)
+            d_probs = dot_t(value, d_out)
+            d_scores = (probs * (d_probs - deltas[h])).astype(BF)
+            d_values.append(dot(probs.astype(BF), d_out))
+            d_keys.append(dot(d_scores, q))
+            dq_acc[:, cs] += dot_l(d_scores, key)
+        dk_all[rows, :] = jnp.concatenate(d_keys, axis=1).astype(BF)
+        dv_all[rows, :] = jnp.concatenate(d_values, axis=1).astype(BF)
+
+    dq_ref[...] = (dq_acc[...] * 0.125).astype(BF)
+    d_key, d_value = dk_all[...], dv_all[...]
+    guk_ref[...] = dot_l(lat_ref[...], d_key).astype(BF)
+    guv_ref[...] = dot_l(lat_ref[...], d_value).astype(BF)
+    term = dot_t(d_key, uk_ref[...]) + dot_t(d_value, uv_ref[...])
+
+    @pl.when(i % 4 == 0)
+    def _():
+        dlat_acc[...] = term
+
+    @pl.when(i % 4 != 0)
+    def _():
+        dlat_acc[...] += term
+
+    @pl.when(i % 4 == 3)
+    def _():
+        dlat_ref[...] = dlat_acc[...].astype(BF)
+
+
+def attend_back(q, k, v, d_heads, mixed, lse, limits, lat_full, u_full):
+    count, keys = q.shape[0], lat_full.shape[0]
+    wide = pl.BlockSpec((count, 128), lambda i: (0, i))
+    tall = pl.BlockSpec((keys, 128), lambda i: (0, i))
+    return pl.pallas_call(
+        attend_back_kernel,
+        name="attend_back",
+        grid=(8,),
+        in_specs=[
+            wide, tall, tall, wide, wide,
+            pl.BlockSpec((1, 2, count), lambda i: (i, 0, 0)),
+            pl.BlockSpec((1, count), lambda i: (0, 0)),
+            pl.BlockSpec((keys, 256), lambda i: (0, i // 4)),
+            pl.BlockSpec((256, 128), lambda i: (0, i)),
+            pl.BlockSpec((256, 128), lambda i: (0, 8 + i)),
+        ],
+        out_specs=[
+            wide,
+            pl.BlockSpec((keys, 256), lambda i: (0, i // 4)),
+            pl.BlockSpec((256, 128), lambda i: (0, i)),
+            pl.BlockSpec((256, 128), lambda i: (0, i)),
+        ],
+        out_shape=[
+            jax.ShapeDtypeStruct((count, 1024), BF),
+            jax.ShapeDtypeStruct((keys, 512), BF),
+            jax.ShapeDtypeStruct((256, 1024), BF),
+            jax.ShapeDtypeStruct((256, 1024), BF),
+        ],
+        scratch_shapes=[
+            pltpu.VMEM((keys, 256), F32),
+            pltpu.VMEM((keys, 128), BF),
+            pltpu.VMEM((keys, 128), BF),
+            pltpu.VMEM((count, 128), F32),
+        ],
+        compiler_params=pltpu.CompilerParams(vmem_limit_bytes=WIDE),
+    )(q, k, v, d_heads, mixed, lse, limits, lat_full, u_full, u_full)
+
+
+def close_kernel(
+    tok, ql, gains, d_resid, dq, dlat,
+    g_ql, g_gain, g_tok,
+    mine, da, db, xb, yb, dh_acc, sends, recvs, locals_,
+):
+    here = Place()
+    here.greet(line=False, sibling=False)
+    s, xs, ys, ds, f = here.s, here.xs, here.ys, here.ds, here.f
+    count = tok.shape[0]
+    half = count // 2
+    w = Wire(sends, recvs, 0)
+    load = pltpu.make_async_copy(dlat, mine, locals_.at[0])
+    load.start()
+    w.send(0, dlat.at[ds, pl.ds(0, half)], da, (ys, f))
+    w.send(1, dlat.at[ds, pl.ds(half, half)], db, (xs, f))
+    normed, inverse = normalize(tok[...].astype(F32))
+    gain = gain_row(gains, 0)
+    h1 = (normed * gain).astype(BF)
+    dh_acc[...] = dot_t(dq[...], ql[:, :1024])
+    load.wait()
+    w.recv(0, da, (ys, f))
+    add_into(mine.at[xs, pl.ds(0, half)], [da])
+    w.send(2, mine.at[xs], xb, (xs, f))
+    w.recv(1, db, (xs, f))
+    add_into(mine.at[ys, pl.ds(half, half)], [db])
+    w.send(3, mine.at[ys], yb, (ys, f))
+    g_ql[:, :1024] = dot_l(h1, dq[...]).astype(BF)
+    w.recv(2, xb, (xs, f))
+    w.recv(3, yb, (ys, f))
+    total = mine[s].astype(F32) + xb[...].astype(F32) + yb[...].astype(F32)
+    d_lat = total.astype(BF)
+    g_ql[:, 1024:] = dot_l(h1, d_lat).astype(BF)
+    dh = dh_acc[...] + dot_t(d_lat, ql[:, 1024:])
+    g_gain[...] = jnp.sum(dh * normed, axis=0, keepdims=True)
+    g_tok[...] = d_resid[...] + norm_back(dh * gain, normed, inverse)
+    w.drain()
+
+
+def close(tok, ql, u_full, d_resid, dq, dlat, collective_id):
+    count = tok.shape[0]
+    return pl.pallas_call(
+        close_kernel,
+        name="close",
+        grid=(1,),
+        in_specs=[
+            vmem(), vmem(),
+            pl.BlockSpec((256, 128), lambda i: (0, 16)),
+            vmem(), vmem(), anywhere(),
+        ],
+        out_specs=[vmem(), vmem(), vmem()],
+        out_shape=[
+            jax.ShapeDtypeStruct((1024, 1536), BF),
+            jax.ShapeDtypeStruct((1, 1024), F32),
+            jax.ShapeDtypeStruct((count, 1024), F32),
+        ],
+        scratch_shapes=[
+            pltpu.VMEM((4, count, 512), BF),
+            pltpu.VMEM((count // 2, 512), BF),
+            pltpu.VMEM((count // 2, 512), BF),
+            pltpu.VMEM((count, 512), BF),
+            pltpu.VMEM((count, 512), BF),
+            pltpu.VMEM((count, 1024), F32),
+            pltpu.SemaphoreType.DMA((1, 4)),
+            pltpu.SemaphoreType.DMA((1, 4)),
+            pltpu.SemaphoreType.DMA((1,)),
+        ],
+        compiler_params=pltpu.CompilerParams(
+            collective_id=collective_id, has_side_effects=True, vmem_limit_bytes=WIDE
+        ),
+    )(tok, ql, u_full, d_resid, dq, dlat)
+
+
+CUTS = {"ql": 16, "u": 8, "wo": 16, "gu": 16, "dn": 48}
+
+
+def quarters(array):
+    rows, cols = array.shape
+    return array.reshape(4, rows // 4, cols)
+
+
+def eighths(array):
+    rows, cols = array.shape
+    return array.reshape(8, 4, rows // 32, cols)
+
+
+def flat(array):
+    return array.reshape(-1, array.shape[-1])
+
+
+def fast_local(
+    tokens, block_ids, gain_attn, w_query, w_latent, up_key, up_value, w_out,
+    gain_ffn, w_gate, w_up, w_down, cotangent,
+):
+    count = tokens.shape[1]
+    x, dy = tokens[0], cotangent[0]
+    gains = jnp.concatenate([gain_attn[None], gain_ffn[None], jnp.zeros((30, 128), BF)])
+    u = jnp.concatenate(
+        [
+            up_key.transpose(1, 0, 2).reshape(32, 1024),
+            up_value.transpose(1, 0, 2).reshape(32, 1024),
+            gains,
+        ],
+        axis=1,
+    )
+    ql = jnp.concatenate([w_query, w_latent], axis=1)
+    gu = jnp.concatenate([w_gate, w_up], axis=1)
+    ql_full, u_full = gather_call(
+        [quarters(ql), quarters(u)], [CUTS["ql"], CUTS["u"]], 0, "gather_attn"
+    )
+    ql_full, u_full = flat(ql_full), flat(u_full)
+    wo_full, gu_full, dn_full = gather_call(
+        [quarters(w_out), quarters(gu), quarters(w_down)],
+        [CUTS["wo"], CUTS["gu"], CUTS["dn"]],
+        1,
+        "gather_ffn",
+    )
+    wo_full, gu_full, dn_full = flat(wo_full), flat(gu_full), flat(dn_full)
+    ids = block_ids[0]
+    own = lax.dynamic_slice_in_dim(ids, lax.axis_index("seq") * count, count)
+    limits = jnp.sum((ids[:, None] <= own[None, :]).astype(jnp.int32), axis=0, keepdims=True)
+
+    q, lat_all = project(x, ql_full, u_full, 2)
+    lat_full = flat(lat_all)
+    mixed, lse, k, v = attend(q, lat_full, u_full, limits)
+    out, d_resid, d_heads, g_wo, g_gain2, g_gu, g_dn = feed(
+        x, dy, mixed, wo_full, u_full, gu_full, dn_full
+    )
+    dq, dlat, g_uk, g_uv = attend_back(q, k, v, d_heads, mixed, lse, limits, lat_full, u_full)
+    g_ql, g_gain1, d_tokens = close(
+        x, ql_full, u_full, d_resid, dq, dlat.reshape(4, count, 512), 3
+    )
+    g_gains = jnp.concatenate(
+        [
+            g_gain1.astype(BF).reshape(8, 1, 128),
+            g_gain2.astype(BF).reshape(8, 1, 128),
+            jnp.zeros((8, 30, 128), BF),
+        ],
+        axis=1,
+    ).reshape(256, 128)
+    g_u = jnp.concatenate([g_uk, g_uv, g_gains], axis=1)
+    r_ql, r_u, r_wo, r_gu, r_dn = reduce_call(
+        [eighths(a) for a in (g_ql, g_u, g_wo, g_gu, g_dn)],
+        [CUTS[n] for n in ("ql", "u", "wo", "gu", "dn")],
+        4,
+        "reduce_all",
+    )
+    r_ql, r_u, r_wo, r_gu, r_dn = (flat(a).astype(F32) for a in (r_ql, r_u, r_wo, r_gu, r_dn))
+    lift = lambda a: a.reshape(32, GROUPS, 512).transpose(1, 0, 2)
+    return (
+        out[None],
+        d_tokens[None],
+        r_u[0, 2048:],
+        r_ql[:, :1024],
+        r_ql[:, 1024:],
+        lift(r_u[:, :1024]),
+        lift(r_u[:, 1024:2048]),
+        r_wo,
+        r_u[1, 2048:],
+        r_gu[:, :2816],
+        r_gu[:, 2816:],
+        r_dn,
+    )
+
+
 def solution(mesh):
     placed = (
         P("fsdp", "seq", None),
@@ -302,8 +1203,9 @@
         P("fsdp", None),
         P("fsdp", "seq", None),
     )
+    tuned = (mesh.shape["seq"], mesh.shape["fsdp"]) == (4, 8)
     return jax.shard_map(
-        local,
+        fast_local if tuned else local,
         mesh=mesh,
         in_specs=placed,
         out_specs=(

time: 1200 us -> 478 us (0.40)
  waiting for transfers between devices: 678 us -> 0 us
  Pallas kernels: 0 us -> 446 us
  matrix products: 346 us -> 0 us
  blocking collectives: 79.9 us -> 0 us
  other arithmetic: 39.3 us -> 11.7 us
  local copies, waits for them, and re-layouts: 30.2 us -> 10.4 us
  between operations: 15.2 us -> 1.1 us
    pallas_call x0 -> x8, Pallas kernels: none -> 446 us  [the longest x1 131 us: reduce_call(): pl.pallas_call(kernel, name=name, out_shape=[jax.ShapeDtypeStruct(a.shape...]
    reduce_scatter x10 -> x0, waiting for transfers between devices: 431 us -> none  [the longest x1 65.4 us: local(): lax.psum_scatter(grad_down.astype(jnp.bfloat16), 'fsdp', scatter_dimensio...]
    dot_general x136 -> x0, matrix products: 346 us -> none  [the longest x32 75.7 us: masked_scores(): jnp.einsum('qd,kd->qk', query_head, key_head, preferred_element_type=jnp....]
    all_gather x8 -> x0, waiting for transfers between devices: 196 us -> none  [the longest x1 52.5 us: local(): lax.all_gather(w_gate, 'fsdp', axis=0, tiled=True)]
    all_gather x4 -> x0, blocking collectives: 56.2 us -> none  [the longest x1 17 us: local(): lax.all_gather(up_value, 'fsdp', axis=1, tiled=True)]
    psum x1 -> x0, waiting for transfers between devices: 46.4 us -> none  [local(): lax.psum(part_query.astype(jnp.bfloat16), 'seq').astype(jnp.float32)]
    unnamed x54 -> x23, local copies, waits for them, and re-layouts: 25 us -> 3.59 us
    convert_element_type x29 -> x5, other arithmetic: 22.3 us -> 3.62 us  [fast_local(): flat(a).astype(F32)]
  transfers between devices with their start and end apart: 19 -> 0, of which waited for: 15 -> 0; matrix products, arithmetic and copies ran while one was open for 16% -> 0% of each run, Pallas kernels for 0% -> 0%
where the time goes in v1:
time: 478 us; the launch traced here: 469 us
  Pallas kernels  446 us (93%)
  other arithmetic  11.7 us (2%)
  local copies, waits for them, and re-layouts  10.4 us (2%)
    pallas_call x1, Pallas kernels, reduce_call(): pl.pallas_call(kernel, name=name, out_shape=[jax.ShapeDtypeStruct(a.shape...  131 us
    pallas_call x2, Pallas kernels, gather_call(): pl.pallas_call(kernel, name=name, out_shape=shapes, in_specs=[pl.BlockSpe...  109 us
    pallas_call x1, Pallas kernels, attend_back(): pl.pallas_call(attend_back_kernel, name='attend_back', grid=(8,), in_spec...  66.4 us
    pallas_call x1, Pallas kernels, feed(): pl.pallas_call(feed_kernel, name='feed', grid=(1,), in_specs=[vmem(), vme...  46.6 us
    pallas_call x1, Pallas kernels, attend(): pl.pallas_call(attend_kernel, name='attend', grid=(8,), in_specs=[pl.Bloc...  39.5 us
    pallas_call x1, Pallas kernels, close(): pl.pallas_call(close_kernel, name='close', grid=(1,), in_specs=[vmem(), v...  27.6 us
    pallas_call x1, Pallas kernels, project(): pl.pallas_call(project_kernel, name='project', grid=(1,), out_shape=[jax....  26.2 us

profile of v1, /device:TPU:0, one launch (start us, length us, event | category | flops | bytes accessed | tf_op | source)
XLA Modules:
  0.0 469.1 jit_solution(13828375530582482671)
XLA Ops:
  0.6 0.0 copy-start.3
  0.7 0.0 copy-start.4
  0.7 0.1 pad.13.clone
  0.8 0.8 constant_dynamic-slice_fusion
  1.5 1.8 convert_reduce_fusion
  3.3 0.7 maximum_bitcast_fusion.1
  4.1 0.9 copy.35
  5.0 0.9 copy.36
  6.0 0.7 pad_maximum_fusion.3.refs_1_
  6.6 1.8 pad_maximum_fusion.2
  8.4 0.0 copy-done.3
  8.4 0.0 copy-done.4
  8.4 1.2 pad_maximum_fusion
  9.6 31.1 %gather_attn.1 = (bf16[8,4,32,1536]{3,2,1,0:T(8,128)(2,1)}, bf16[8,4,8,2176]{3,2,1,0:T(8,128)(2,1)}) custom-call(bf16[4,32,1536]{2,1,0:T(8,128)(2,1)} %bitcast.81, bf16[4,8,2176]{2,1,0:T(8,128)(2,1)} %pad_maximum_fusion.3.refs_1_), custom_call_target="tpu_custom_call" | custom-call | tf_op jit(solution)/shard_map/gather_attn/pallas_call | solution.py:482
  40.8 26.2 %project.1 = (bf16[512,1024]{1,0:T(8,128)(2,1)}, bf16[4,512,512]{2,1,0:T(8,128)(2,1)}) custom-call(bf16[512,1024]{1,0:T(8,128)(2,1)} %bitcast.68, bf16[1024,1536]{1,0:T(8,128)(2,1)} %bitcast.64, bf16[256,2176]{1,0:T(8,128)(2,1)} %bitcast.57), custom_call_target="tpu_custom_call" | custom-call | tf_op jit(solution)/shard_map/project/pallas_call | solution.py:739
  66.9 39.5 %attend.1 = (bf16[512,1024]{1,0:T(8,128)(2,1)}, f32[8,2,512]{2,1,0:T(2,128)}, bf16[2048,1024]{1,0:T(8,128)(2,1)}, bf16[2048,1024]{1,0:T(8,128)(2,1)}) custom-call(bf16[512,1024]{1,0:T(8,128)(2,1)} %get-tuple-element.44.q_ref, bf16[2048,512]{1,0:T(8,128)(2,1)} %bitcast.71, bf16[256,2176]{1,0:T(8,128)(2,1)} %bitcast.58, bf16[256,2176]{1,0:T(8,128)(2,1)} %bitcast.59, ...), custom_call_target="tpu_custom_call" | custom-call | tf_op jit(solution)/shard_map/attend/pallas_call | solution.py:785
  106.5 77.9 %gather_ffn.1 = (bf16[8,4,32,1024]{3,2,1,0:T(8,128)(2,1)}, bf16[8,4,32,5632]{3,2,1,0:T(8,128)(2,1)}, bf16[8,4,88,1024]{3,2,1,0:T(8,128)(2,1)}) custom-call(bf16[4,32,1024]{2,1,0:T(8,128)(2,1)} %bitcast.88, bf16[4,32,5632]{2,1,0:T(8,128)(2,1)} %bitcast.73, bf16[4,88,1024]{2,1,0:T(8,128)(2,1)} %bitcast.83), custom_call_target="tpu_custom_call" | custom-call | tf_op jit(solution)/shard_map/gather_ffn/pallas_call | solution.py:482
  184.4 46.6 %feed.1 = (bf16[512,1024]{1,0:T(8,128)(2,1)}, f32[512,1024]{1,0:T(8,128)}, bf16[512,1024]{1,0:T(8,128)(2,1)}, bf16[1024,1024]{1,0:T(8,128)(2,1)}, f32[1,1024]{1,...) custom-call(bf16[512,1024]{1,0:T(8,128)(2,1)} %bitcast.69, bf16[512,1024]{1,0:T(8,128)(2,1)} %bitcast.82, ...), custom_call_target="tpu_custom_call" | custom-call | tf_op jit(solution)/shard_map/feed/pallas_call | solution.py:897
  231.0 66.4 %attend_back.1 = (bf16[512,1024]{1,0:T(8,128)(2,1)}, bf16[2048,512]{1,0:T(8,128)(2,1)}, bf16[256,1024]{1,0:T(8,128)(2,1)}, bf16[256,1024]{1,0:T(8,128)(2,1)}) custom-call(bf16[512,1024]{1,0:T(8,128)(2,1)} %get-tuple-element.44.q_ref, bf16[2048,1024]{1,0:T(8,128)(2,1)} %get-tuple-element.52.k_ref, bf16[2048,1024]{1,0:T(8,128)(2,1)} %get-tuple-element.53.v_ref, ...), custom_call_target="tpu_custom_call" | custom-call | tf_op jit(solution)/shard_map/attend_back/pallas_call | solution.py:992
  297.4 0.0 copy-start.9
  297.4 0.0 copy-start.5
  297.4 0.0 copy-start.6
  297.4 27.6 %close.1 = (bf16[1024,1536]{1,0:T(8,128)(2,1)}, f32[1,1024]{1,0:T(1,128)}, f32[512,1024]{1,0:T(8,128)}) custom-call(bf16[512,1024]{1,0:T(8,128)(2,1)} %bitcast.70, bf16[1024,1536]{1,0:T(8,128)(2,1)} %bitcast.65, bf16[256,2176]{1,0:T(8,128)(2,1)} %bitcast.63, f32[512,1024]{1,0:T(8,128)} %get-tuple-element.51.d_resid, bf16[512,1024]{1,0:T(8,128)(2,1)} %get-tuple-element.56.dq, ...), custom_call_target="tpu_custom_call" | custom-call | tf_op jit(solution)/shard_map/close/pallas_call | solution.py:1066
  325.1 0.0 copy-done.9
  325.1 0.7 convert_bitcast_fusion
  325.7 0.1 maximum_bitcast_fusion
  325.8 0.0 copy-done.5
  325.8 0.0 copy-done.6
  325.9 1.1 pad_maximum_fusion.1.refs_1_
  326.9 130.6 %reduce_all.1 = (bf16[4,32,1536]{2,1,0:T(8,128)(2,1)}, bf16[4,8,2176]{2,1,0:T(8,128)(2,1)}, bf16[4,32,1024]{2,1,0:T(8,128)(2,1)}, bf16[4,32,5632]{2,1,0:T(8,128)(2,1)}, bf16[4,88,1024]{2,1,0:T(8,128)(2,1)}) custom-call(bf16[8,4,32,1536]{3,2,1,0:T(8,128)(2,1)} %bitcast.76, bf16[8,4,8,2176]{3,2,1,0:T(8,128)(2,1)} %pad_maximum_fusion.1.refs_1_, ...), custom_call_target="tpu_custom_call" | custom-call | tf_op jit(solution)/shard_map/reduce_all/pallas_call | solution.py:684
  457.5 0.0 copy-start.8
  457.5 0.0 copy-start.7
  457.5 1.0 bitcast_convert_fusion.4
  458.5 0.5 slice_bitcast_fusion
  459.1 0.1 reshape.131
  459.2 0.7 copy.40
  459.9 0.0 copy-start.2
  459.9 0.1 reshape.130
  460.0 0.7 copy.39
  460.7 0.0 copy-done.8
  460.7 0.9 bitcast_convert_fusion.3
  461.5 0.0 copy-done.7
  461.5 0.1 bitcast_convert_fusion.2
  461.6 0.0 copy-start.1
  461.6 0.7 slice.34
  462.4 0.8 slice.33
  463.2 0.0 copy-done.2
  463.2 1.3 bitcast_convert_fusion.1
  464.5 0.0 copy-done.1
  464.5 0.4 bitcast_convert_fusion
  464.9 0.0 copy-start
  464.9 1.8 fusion
  466.7 0.9 copy-done
  467.5 1.3 copy.42
  (4 shorter events, 0.1 us)
Async XLA Ops:
  0.6 7.8 %copy-start.3 = (bf16[128,2816]{1,0:T(8,128)(2,1)S(1)}, bf16[128,2816]{1,0:T(8,128)(2,1)}, u32[]{:S(2)}) copy-start(bf16[128,2816]{1,0:T(8,128)(2,1)} %param.23) | copy-start | bytes 2162692
  0.7 7.8 %copy-start.4 = (bf16[128,2816]{1,0:T(8,128)(2,1)S(1)}, bf16[128,2816]{1,0:T(8,128)(2,1)}, u32[]{:S(2)}) copy-start(bf16[128,2816]{1,0:T(8,128)(2,1)} %param.22) | copy-start | bytes 2162692
  297.4 27.7 %copy-start.9 = (f32[1,1024]{1,0:T(1,128)S(1)}, f32[1,1024]{1,0:T(1,128)}, u32[]{:S(2)}) copy-start(f32[1,1024]{1,0:T(1,128)} %get-tuple-element.63) | copy-start | bytes 12292
  297.4 28.4 %copy-start.5 = (bf16[256,1024]{1,0:T(8,128)(2,1)S(1)}, bf16[256,1024]{1,0:T(8,128)(2,1)}, u32[]{:S(2)}) copy-start(bf16[256,1024]{1,0:T(8,128)(2,1)} %get-tuple-element.60) | copy-start | bytes 1572868
  297.4 28.4 %copy-start.6 = (bf16[256,1024]{1,0:T(8,128)(2,1)S(1)}, bf16[256,1024]{1,0:T(8,128)(2,1)}, u32[]{:S(2)}) copy-start(bf16[256,1024]{1,0:T(8,128)(2,1)} %get-tuple-element.61) | copy-start | bytes 1572868
  457.5 3.1 copy-start.8
  457.5 4.0 copy-start.7
  459.9 3.3 copy-start.2
  461.6 2.9 copy-start.1
  464.9 2.6 copy-start

commit v2 on v0

--- a/solution.py
+++ b/solution.py
@@ -1,6 +1,8 @@
 import jax
 import jax.numpy as jnp
 from jax import lax
+from jax.experimental import pallas as pl
+from jax.experimental.pallas import tpu as pltpu
 from jax.sharding import PartitionSpec as P
 
 HEADS = 16
@@ -286,6 +288,1170 @@
     )
 
 
+MESH = pl.DeviceIdType.MESH
+NEG = -1e30
+WIDE = 60 * 2**20
+BF = jnp.bfloat16
+F32 = jnp.float32
+CUTS = {"wo": 16, "gu": 16, "dn": 48}
+
+
+def dot(a, b):
+    return jnp.dot(a, b, preferred_element_type=F32)
+
+
+def dot_t(a, b):
+    return lax.dot_general(a, b, (((1,), (1,)), ((), ())), preferred_element_type=F32)
+
+
+def dot_l(a, b):
+    return lax.dot_general(a, b, (((0,), (0,)), ((), ())), preferred_element_type=F32)
+
+
+class Place:
+    def __init__(self):
+        s, f = lax.axis_index("seq"), lax.axis_index("fsdp")
+        self.s, self.f = s, f
+        self.z, self.c = lax.div(f, 2), lax.rem(f, 2)
+        self.xs = s + 1 - 2 * lax.rem(s, 2)
+        self.ys = s + 2 - 4 * lax.div(s, 2)
+        self.ds = 3 - s
+        self.sib = f + 1 - 2 * self.c
+        self.half = lax.div(self.z, 2)
+        self.inner = lax.rem(lax.div(self.z + 1, 2), 2)
+
+    def greet(self, line=True, sibling=True):
+        bar = pltpu.get_barrier_semaphore()
+
+        def hail(seq, fsdp):
+            pl.semaphore_signal(bar, inc=1, device_id=(seq, fsdp), device_id_type=MESH)
+
+        hail(self.xs, self.f)
+        hail(self.ys, self.f)
+        count = 2
+        if sibling:
+            hail(self.s, self.sib)
+            count = count + 1
+        if line:
+            for d in (1, 2, 3):
+                hail(self.s, lax.rem(self.f + 2 * d, 8))
+            count = count + 3
+        pl.semaphore_wait(bar, count)
+
+
+class Wire:
+    def __init__(self, sends, recvs, tensor):
+        self.sends, self.recvs, self.tensor = sends, recvs, tensor
+        self.draining = False
+
+    def copy(self, kind, src, dst, dev):
+        return pltpu.make_async_remote_copy(
+            src_ref=src,
+            dst_ref=dst,
+            send_sem=self.sends.at[self.tensor, kind],
+            recv_sem=self.recvs.at[self.tensor, kind],
+            device_id=dev,
+            device_id_type=MESH,
+        )
+
+    def send(self, kind, src, dst, dev):
+        copy = self.copy(kind, src, dst, dev)
+        if self.draining:
+            copy.wait_send()
+        else:
+            copy.start()
+
+    def recv(self, kind, landing, dev):
+        if not self.draining:
+            self.copy(kind, landing, landing, dev).wait_recv()
+
+
+class Gather:
+    KINDS = 37
+
+    def __init__(self, here, shards, fulls, cuts, sends, recvs, locals_, relay):
+        self.here, self.locals, self.relay = here, locals_, relay
+        self.each = [
+            (t, Wire(sends, recvs, t), shards[t], fulls[t], cuts[t]) for t in range(len(shards))
+        ]
+
+    def rows(self, full, f, p=None, lo=0, n=None):
+        size = full.shape[0] // 8
+        start = f * size
+        if p is not None:
+            start = start + p * (size // 4)
+            size = size // 4
+        return full.at[pl.ds(pl.multiple_of(start + lo, 8), size - lo if n is None else n)]
+
+    def slot(self, way, d):
+        h = self.here
+        j = way * 3 + d - 1
+        if way == 0:
+            return j, h.z >= d, h.f - 2 * d
+        return j, h.z + d <= 3, h.f + 2 * d
+
+    def own(self, t, shard, full):
+        return pltpu.make_async_copy(shard, self.rows(full, self.here.f), self.locals.at[t])
+
+    def piece(self, full, f, cut):
+        return self.rows(full, f, None if cut is None else self.here.s)
+
+    def go(self, d):
+        h = self.here
+        for t, w, shard, full, cut in self.each:
+            there = self.piece(full, h.f, cut)
+            if cut is None:
+                mine = shard
+            else:
+                q = shard.shape[0] // 4
+                mine = shard.at[pl.ds(pl.multiple_of(h.s * q, 8), q)]
+            pl.when(h.z + d <= 3)(lambda: w.send(d - 1, mine, there, (h.s, h.f + 2 * d)))
+            pl.when(h.z >= d)(lambda: w.send(d + 2, mine, there, (h.s, h.f - 2 * d)))
+
+    def near(self):
+        h = self.here
+        for t, w, shard, full, cut in self.each:
+            w.send(36, shard, self.rows(full, h.f), (h.s, h.sib))
+            if not w.draining:
+                self.own(t, shard, full).start()
+
+    def line(self, d):
+        h = self.here
+        for way in range(2):
+            j, act, fp = self.slot(way, d)
+            more = h.z < 3 if way == 0 else h.z > 0
+            for t, w, shard, full, cut in self.each:
+                piece = self.piece(full, fp, cut)
+
+                @pl.when(act)
+                def _():
+                    w.recv(j, piece, (h.s, h.f))
+                    if self.relay and d < 3:
+                        onward = h.f + 2 - 4 * way
+                        pl.when(more)(lambda: w.send(j + 1, piece, piece, (h.s, onward)))
+
+    def plane(self, d):
+        h = self.here
+        for way in range(2):
+            j, act, fp = self.slot(way, d)
+            for t, w, shard, full, cut in self.each:
+                if cut is None:
+                    continue
+                piece = self.piece(full, fp, cut)
+
+                @pl.when(act)
+                def _():
+                    w.send(6 + j, piece, piece, (h.xs, h.f))
+                    w.send(12 + j, piece, piece, (h.ys, h.f))
+
+    def turn(self, d):
+        h = self.here
+        for way in range(2):
+            j, act, fp = self.slot(way, d)
+            for t, w, shard, full, cut in self.each:
+                if cut is None:
+                    continue
+                q = shard.shape[0] // 4
+                top, low = self.rows(full, fp, h.xs), self.rows(full, fp, h.ys)
+                part = self.rows(full, fp, h.xs, 0, cut)
+                rest = self.rows(full, fp, h.ys, cut) if cut < q else None
+
+                @pl.when(act)
+                def _():
+                    w.recv(6 + j, top, (h.xs, h.f))
+                    w.send(18 + j, part, part, (h.ys, h.f))
+                    w.recv(12 + j, low, (h.ys, h.f))
+                    if cut < q:
+                        w.send(24 + j, rest, rest, (h.xs, h.f))
+
+    def cross(self, d):
+        h = self.here
+        for way in range(2):
+            j, act, fp = self.slot(way, d)
+            for t, w, shard, full, cut in self.each:
+                whole = self.rows(full, fp)
+
+                @pl.when(act)
+                def _():
+                    if cut is not None:
+                        w.recv(18 + j, self.rows(full, fp, h.ds, 0, cut), (h.ys, h.f))
+                        if cut < shard.shape[0] // 4:
+                            w.recv(24 + j, self.rows(full, fp, h.ds, cut), (h.xs, h.f))
+                    w.send(30 + j, whole, whole, (h.s, h.sib))
+
+    def arrive(self):
+        h = self.here
+        for t, w, shard, full, cut in self.each:
+            w.recv(36, self.rows(full, h.sib), (h.s, h.sib))
+            for way in range(2):
+                for d in (1, 2, 3):
+                    j, act, fp = self.slot(way, d)
+                    theirs = self.rows(full, fp + 1 - 2 * h.c)
+                    pl.when(act)(lambda: w.recv(30 + j, theirs, (h.s, h.sib)))
+            self.own(t, shard, full).wait()
+
+    def drain(self):
+        for t, w, shard, full, cut in self.each:
+            w.draining = True
+        self.near()
+        for d in (1, 2, 3):
+            if d == 1 or not self.relay:
+                self.go(d)
+            self.line(d)
+            self.plane(d)
+            self.turn(d)
+            self.cross(d)
+        for t, w, shard, full, cut in self.each:
+            w.draining = False
+
+    @staticmethod
+    def sems(count):
+        return [
+            pltpu.SemaphoreType.DMA((count, Gather.KINDS)),
+            pltpu.SemaphoreType.DMA((count, Gather.KINDS)),
+            pltpu.SemaphoreType.DMA((count,)),
+        ]
+
+
+def rows_of(q):
+    return 16 if q % 16 == 0 else q
+
+
+def add_into(target, others):
+    q = target.shape[0]
+    step = rows_of(q)
+
+    def body(r):
+        total = target[r, :].astype(F32)
+        for other in others:
+            total = total + other[r, :].astype(F32)
+        target[r, :] = total.astype(target.dtype)
+
+    if step == q:
+        body(slice(0, q))
+    else:
+
+        @pl.loop(0, q // step)
+        def _(k):
+            body(pl.ds(pl.multiple_of(k * step, step), step))
+
+
+class Reduce:
+    KINDS = 28
+    REFS = 7
+
+    @staticmethod
+    def scratch(shapes, cuts, ways):
+        out = []
+        for (q, cols), cut, way in zip(shapes, cuts, ways):
+            n = 4 if way == "plane" else 1
+            zs = (2, 4, q, cols) if way == "plane" else (6, 4, q, cols)
+            out += [
+                pltpu.VMEM((4, 4, q, cols), BF),
+                pltpu.VMEM((4, 4, q, cols), BF),
+                pltpu.VMEM((n, cut, cols), BF),
+                pltpu.VMEM((n, max(q - cut, 8), cols), BF),
+                pltpu.VMEM((n, q, cols), BF),
+                pltpu.VMEM((n, q, cols), BF),
+                pltpu.VMEM(zs, BF),
+            ]
+        n = len(shapes)
+        return out + [
+            pltpu.SemaphoreType.DMA((n, Reduce.KINDS)),
+            pltpu.SemaphoreType.DMA((n, Reduce.KINDS)),
+            pltpu.SemaphoreType.DMA((n, 4)),
+        ]
+
+    def __init__(self, here, parts, cuts, ways, scratch):
+        n, k = len(parts), Reduce.REFS
+        sends, recvs, self.locals = scratch[k * n :]
+        self.here = here
+        self.each = [
+            (t, Wire(sends, recvs, t), parts[t], cuts[t], ways[t]) + tuple(scratch[k * t : k * t + k])
+            for t in range(n)
+        ]
+
+    def target(self, i):
+        h = self.here
+        if i < 2:
+            return 3 - 3 * h.half + i * (2 * h.half - 1)
+        return 1 - h.z + 4 * h.half if i == 2 else h.z
+
+    def result(self, t):
+        return self.each[t][5].at[3, self.here.s]
+
+    def load(self, t, part, acc, i):
+        return pltpu.make_async_copy(
+            part.at[2 * self.target(i) + self.here.c], acc.at[i], self.locals.at[t, i]
+        )
+
+    def start(self, which=None):
+        h = self.here
+        for i in range(4):
+            for t, w, part, cut, way, acc, sib, *_ in self.each:
+                if which is None or t in which:
+                    w.send(i, part.at[2 * self.target(i) + 1 - h.c], sib.at[i], (h.s, h.sib))
+                    if not w.draining:
+                        self.load(t, part, acc, i).start()
+
+    def pair(self, i, which=None):
+        for t, w, part, cut, way, acc, sib, da, db, xb, yb, zb in self.each:
+            if which is not None and t not in which:
+                continue
+            if not w.draining:
+                self.load(t, part, acc, i).wait()
+                w.recv(i, sib.at[i], (self.here.s, self.here.sib))
+                for p in range(4):
+                    add_into(acc.at[i, p], [sib.at[i, p]])
+            if way == "plane":
+                self.corner(t, i)
+
+    def corner(self, t, i):
+        h = self.here
+        t, w, part, cut, way, acc, sib, da, db, xb, yb, zb = self.each[t]
+        q, n = acc.shape[2], (i if way == "plane" else 0)
+        w.send(4 + i, acc.at[i, h.ds, pl.ds(0, cut)], da.at[n], (h.ys, h.f))
+        if cut < q:
+            w.send(8 + i, acc.at[i, h.ds, pl.ds(cut, q - cut)], db.at[n], (h.xs, h.f))
+
+    def turn(self, i, which=None):
+        h = self.here
+        for t, w, part, cut, way, acc, sib, da, db, xb, yb, zb in self.each:
+            if which is not None and t not in which:
+                continue
+            q, n = acc.shape[2], (i if way == "plane" else 0)
+            if not w.draining:
+                w.recv(4 + i, da.at[n], (h.ys, h.f))
+                add_into(acc.at[i, h.xs, pl.ds(0, cut)], [da.at[n]])
+                if cut < q:
+                    w.recv(8 + i, db.at[n], (h.xs, h.f))
+                    add_into(acc.at[i, h.ys, pl.ds(cut, q - cut)], [db.at[n]])
+            w.send(12 + i, acc.at[i, h.xs], xb.at[n], (h.xs, h.f))
+            w.send(16 + i, acc.at[i, h.ys], yb.at[n], (h.ys, h.f))
+
+    def meet(self, i, which=None):
+        h = self.here
+        for t, w, part, cut, way, acc, sib, da, db, xb, yb, zb in self.each:
+            if which is not None and t not in which:
+                continue
+            n = i if way == "plane" else 0
+            w.recv(12 + i, xb.at[n], (h.xs, h.f))
+            w.recv(16 + i, yb.at[n], (h.ys, h.f))
+            add_into(acc.at[i, h.s], [xb.at[n], yb.at[n]])
+
+    def line(self, i, which=None, role=None):
+        h = self.here
+        zp = self.target(i)
+        up = h.half if i < 2 else lax.rem(h.half + h.inner, 2)
+        for t, w, part, cut, way, acc, sib, da, db, xb, yb, zb in self.each:
+            if which is not None and t not in which:
+                continue
+            if way == "plane":
+                mine, land = acc.at[i, h.s], lambda u, z: zb.at[u, z]
+                add = lambda ref: add_into(mine, [ref])
+            else:
+                mine, land = acc.at[i], lambda u, z: zb.at[z - 1 + 4 * u]
+
+                def add(ref):
+                    for p in range(4):
+                        add_into(mine.at[p], [ref.at[p]])
+
+            if i < 3:
+
+                def pass_on():
+                    w.send(20 + up * 4 + zp, mine, land(up, zp), (h.s, h.f + 2 - 4 * up))
+
+                if w.draining:
+                    pass_on()
+                    continue
+
+                if role != 0:
+
+                    @pl.when(h.inner == 1)
+                    def _():
+                        w.recv(20 + up * 4 + zp, land(up, zp), (h.s, h.f))
+                        add(land(up, zp))
+                        pass_on()
+
+                if role != 1:
+                    pl.when(h.inner == 0)(pass_on)
+            elif not w.draining:
+
+                @pl.when(h.z > 0)
+                def _():
+                    w.recv(20 + zp, land(0, zp), (h.s, h.f))
+                    add(land(0, zp))
+
+                @pl.when(h.z < 3)
+                def _():
+                    w.recv(24 + zp, land(1, zp), (h.s, h.f))
+                    add(land(1, zp))
+
+    def drain(self):
+        for t, w, *_ in self.each:
+            w.draining = True
+        self.start()
+        for i in range(4):
+            self.pair(i)
+            self.turn(i, [t for t, e in enumerate(self.each) if e[4] == "plane" or i == 3])
+            self.line(i)
+        for t, e in enumerate(self.each):
+            if e[4] == "line":
+                self.corner(t, 3)
+        for t, w, *_ in self.each:
+            w.draining = False
+
+
+class Share:
+    def __init__(self, here, quarters, outs, cuts, sends, recvs, locals_):
+        self.here, self.locals = here, locals_
+        self.each = [
+            (t, Wire(sends, recvs, t), quarters[t], outs[t], cuts[t]) for t in range(len(outs))
+        ]
+
+    @staticmethod
+    def sems(count):
+        return [
+            pltpu.SemaphoreType.DMA((count, 4)),
+            pltpu.SemaphoreType.DMA((count, 4)),
+            pltpu.SemaphoreType.DMA((count,)),
+        ]
+
+    def own(self, t, quarter, out):
+        return pltpu.make_async_copy(quarter, out.at[self.here.s], self.locals.at[t])
+
+    def start(self):
+        h = self.here
+        for t, w, quarter, out, cut in self.each:
+            w.send(0, quarter, out.at[h.s], (h.xs, h.f))
+            w.send(1, quarter, out.at[h.s], (h.ys, h.f))
+            if not w.draining:
+                self.own(t, quarter, out).start()
+
+    def turn(self):
+        h = self.here
+        for t, w, quarter, out, cut in self.each:
+            q = out.shape[1]
+            w.recv(0, out.at[h.xs], (h.xs, h.f))
+            piece = out.at[h.xs, pl.ds(0, cut)]
+            w.send(2, piece, piece, (h.ys, h.f))
+            w.recv(1, out.at[h.ys], (h.ys, h.f))
+            if cut < q:
+                piece = out.at[h.ys, pl.ds(cut, q - cut)]
+                w.send(3, piece, piece, (h.xs, h.f))
+
+    def arrive(self):
+        h = self.here
+        for t, w, quarter, out, cut in self.each:
+            q = out.shape[1]
+            w.recv(2, out.at[h.ds, pl.ds(0, cut)], (h.ys, h.f))
+            if cut < q:
+                w.recv(3, out.at[h.ds, pl.ds(cut, q - cut)], (h.xs, h.f))
+            self.own(t, quarter, out).wait()
+
+    def drain(self):
+        for t, w, *_ in self.each:
+            w.draining = True
+        self.start()
+        self.turn()
+
+
+def gain_row(block, which):
+    rows = [block[128 * f + which : 128 * f + which + 1, :] for f in range(8)]
+    return jnp.concatenate(rows, axis=1).astype(F32)
+
+
+def vmem():
+    return pl.BlockSpec(memory_space=pltpu.VMEM)
+
+
+def anywhere():
+    return pl.BlockSpec(memory_space=pl.ANY)
+
+
+def attend_pair(q, k_ref, v_ref, lim, o_ref, lse_ref, between):
+    outs = []
+    for h in range(2):
+        if h == 1:
+            between()
+        cs = slice(64 * h, 64 * h + 64)
+        scores = dot_t(k_ref[:, cs], q[:, cs] * jnp.asarray(0.125, BF))
+        allowed = lax.broadcasted_iota(jnp.int32, scores.shape, 0) < lim
+        scores = jnp.where(allowed, scores, NEG)
+        peak = jnp.max(scores, axis=0, keepdims=True)
+        shifted = jnp.exp(scores - peak)
+        total = jnp.sum(shifted, axis=0, keepdims=True)
+        outs.append(dot_l(v_ref[:, cs], shifted.astype(BF)) / total)
+        lse_ref[0, h : h + 1, :] = peak + jnp.log(total)
+    o_ref[...] = jnp.concatenate(outs, axis=0).T.astype(BF)
+
+
+def open_kernel(
+    tok, lim, wl_s, wq_s, u_s, gu_s, dn_s, wo_s,
+    mixed, lse, k_out, v_out, q_out, lat_out, wl_full, wq_full, u_full, gu_full, dn_full, wo_full,
+    qs, lat, wl, wq, u, h1_ref,
+    a_send, a_recv, a_loc, b_send, b_recv, b_loc, f_send, f_recv, f_loc, o_send, o_recv, o_loc,
+    l_send, l_recv, l_loc,
+):
+    i = pl.program_id(0)
+    here = Place()
+    s, xs, ys, ds, f = here.s, here.xs, here.ys, here.ds, here.f
+    one = Gather(here, [wl_s], [wl], [16], a_send, a_recv, a_loc, False)
+    two = Gather(here, [wq_s, u_s], [wq, u_full], [16, 8], b_send, b_recv, b_loc, False)
+    ffn = Gather(here, [gu_s, dn_s], [gu_full, dn_full], [16, 48], f_send, f_recv, f_loc, True)
+    last = Gather(here, [wo_s], [wo_full], [None], o_send, o_recv, o_loc, True)
+    keep_wl = pltpu.make_async_copy(wl, wl_full, l_loc.at[0])
+    keep_lat = pltpu.make_async_copy(lat, lat_out, l_loc.at[1])
+    fetch_u = pltpu.make_async_copy(u_full, u, l_loc.at[2])
+    keep_wq = pltpu.make_async_copy(wq, wq_full, l_loc.at[3])
+    count = tok.shape[0]
+    half = count // 2
+    wires = [Wire(l_send, l_recv, g) for g in range(2)]
+
+    def lat_out_of(g):
+        wires[g].send(0, lat.at[g, s], lat.at[g, s], (xs, f))
+        wires[g].send(1, lat.at[g, s], lat.at[g, s], (ys, f))
+
+    def lat_turn(g):
+        wires[g].recv(0, lat.at[g, xs], (xs, f))
+        top = lat.at[g, xs, pl.ds(0, half)]
+        wires[g].send(2, top, top, (ys, f))
+        wires[g].recv(1, lat.at[g, ys], (ys, f))
+        low = lat.at[g, ys, pl.ds(half, half)]
+        wires[g].send(3, low, low, (xs, f))
+
+    def lat_end(g):
+        wires[g].recv(2, lat.at[g, ds, pl.ds(0, half)], (ys, f))
+        wires[g].recv(3, lat.at[g, ds, pl.ds(half, half)], (xs, f))
+
+    @pl.when(i == 0)
+    def _():
+        here.greet()
+        for gather in (one, two):
+            for d in (1, 2, 3):
+                gather.go(d)
+            gather.near()
+        normed, _ = normalize(tok[...].astype(F32))
+        for d in (1, 2, 3):
+            one.line(d)
+            one.plane(d)
+        two.line(1)
+        two.plane(1)
+        ffn.go(1)
+        for d in (1, 2, 3):
+            one.turn(d)
+        ffn.near()
+        for d in (2, 3):
+            two.line(d)
+            two.plane(d)
+        for d in (1, 2, 3):
+            one.cross(d)
+        two.turn(1)
+        one.arrive()
+        h1_ref[...] = (normed * gain_row(wl[:, 512:], 0)).astype(BF)
+        h1 = h1_ref[...]
+        keep_wl.start()
+        lat[0, s] = dot(h1, wl[:, :256]).astype(BF)
+        lat_out_of(0)
+        ffn.line(1)
+        two.turn(2)
+        two.turn(3)
+        lat[1, s] = dot(h1, wl[:, 256:512]).astype(BF)
+        for d in (1, 2, 3):
+            two.cross(d)
+        lat_turn(0)
+        lat_out_of(1)
+        two.arrive()
+        fetch_u.start()
+        keep_wq.start()
+        for p in range(8):
+            qs[p] = dot(h1, wq[:, 128 * p : 128 * p + 128]).astype(BF)
+        ffn.plane(1)
+        ffn.line(2)
+        fetch_u.wait()
+        lat_end(0)
+
+    plan = {
+        (1, 0): [lambda: lat_turn(1)],
+        (1, 1): [lambda: ffn.plane(2)],
+        (2, 1): [lambda: ffn.line(3), lambda: last.near(), lambda: last.go(1)],
+        (3, 0): [lambda: ffn.turn(1), lambda: ffn.plane(3)],
+        (4, 0): [lambda: lat_end(1), lambda: keep_lat.start(), lambda: last.line(1)],
+        (5, 0): [lambda: ffn.cross(1)],
+        (5, 1): [lambda: last.line(2), lambda: ffn.turn(2)],
+        (6, 1): [lambda: ffn.cross(2)],
+        (7, 0): [lambda: last.line(3)],
+        (7, 1): [lambda: ffn.turn(3), lambda: [last.cross(d) for d in (1, 2, 3)]],
+    }
+
+    def at(h):
+        for (step, part), acts in plan.items():
+            if part == h:
+
+                @pl.when(i == step)
+                def _():
+                    for act in acts:
+                        act()
+
+    at(0)
+    q = qs[i]
+    q_out[...] = q
+    cols = pl.multiple_of(i * 128, 128)
+    latents = lat[lax.div(i, 4)].reshape(4 * count, 256)
+    k_out[...] = dot(latents, u[:, pl.ds(cols, 128)]).astype(BF)
+    v_out[...] = dot(latents, u[:, pl.ds(1024 + cols, 128)]).astype(BF)
+    attend_pair(q, k_out, v_out, lim[...], mixed, lse, lambda: at(1))
+
+    @pl.when(i == 7)
+    def _():
+        ffn.cross(3)
+        last.arrive()
+        ffn.arrive()
+        keep_wl.wait()
+        keep_wq.wait()
+        keep_lat.wait()
+        for gather in (one, two, ffn, last):
+            gather.drain()
+        for g in range(2):
+            wires[g].draining = True
+            lat_out_of(g)
+            lat_turn(g)
+
+
+def open_call(tok, limits, wl, wq, u, gu, dn, wo, collective_id):
+    count = tok.shape[0]
+    keys = 4 * count
+    block = lambda n: pl.BlockSpec((n, 128), lambda i: (0, i))
+    full = lambda a: jax.ShapeDtypeStruct((8 * a.shape[0], a.shape[1]), a.dtype)
+    return pl.pallas_call(
+        open_kernel,
+        name="open",
+        grid=(8,),
+        in_specs=[
+            pl.BlockSpec((count, 1024), lambda i: (0, 0)),
+            pl.BlockSpec((1, count), lambda i: (0, 0)),
+        ]
+        + [anywhere()] * 6,
+        out_specs=[
+            block(count),
+            pl.BlockSpec((1, 2, count), lambda i: (i, 0, 0)),
+            block(keys),
+            block(keys),
+            block(count),
+        ]
+        + [anywhere()] * 7,
+        out_shape=[
+            jax.ShapeDtypeStruct((count, 1024), BF),
+            jax.ShapeDtypeStruct((8, 2, count), F32),
+            jax.ShapeDtypeStruct((keys, 1024), BF),
+            jax.ShapeDtypeStruct((keys, 1024), BF),
+            jax.ShapeDtypeStruct((count, 1024), BF),
+            jax.ShapeDtypeStruct((2, 4, count, 256), BF),
+        ]
+        + [full(a) for a in (wl, wq, u, gu, dn, wo)],
+        scratch_shapes=[
+            pltpu.VMEM((8, count, 128), BF),
+            pltpu.VMEM((2, 4, count, 256), BF),
+            pltpu.VMEM((1024, 640), BF),
+            pltpu.VMEM((1024, 1024), BF),
+            pltpu.VMEM((256, 2048), BF),
+            pltpu.VMEM((count, 1024), BF),
+        ]
+        + Gather.sems(1)
+        + Gather.sems(2)
+        + Gather.sems(2)
+        + Gather.sems(1)
+        + [
+            pltpu.SemaphoreType.DMA((2, 4)),
+            pltpu.SemaphoreType.DMA((2, 4)),
+            pltpu.SemaphoreType.DMA((4,)),
+        ],
+        compiler_params=pltpu.CompilerParams(
+            collective_id=collective_id, has_side_effects=True, vmem_limit_bytes=WIDE
+        ),
+    )(tok, limits, wl, wq, u, gu, dn, wo)
+
+
+FF_TILES = ((0, 768), (768, 768), (1536, 640), (2176, 640))
+
+
+def feed_kernel(
+    tok, cot, mixed, wo, gains, gu, dn,
+    out, d_resid, d_heads, g_wo, g_gain, g_gu, g_dn,
+    wg, wu, wd, gg, gup, gd, h2_ref, y_acc, dh_acc, in_sems, out_sems,
+):
+    ff = dn.shape[0]
+
+    def fetch(j):
+        lo, n = FF_TILES[j]
+        b = j % 2
+        return [
+            pltpu.make_async_copy(gu.at[:, pl.ds(lo, n)], wg.at[b, :, pl.ds(0, n)], in_sems.at[b, 0]),
+            pltpu.make_async_copy(gu.at[:, pl.ds(ff + lo, n)], wu.at[b, :, pl.ds(0, n)], in_sems.at[b, 1]),
+            pltpu.make_async_copy(dn.at[pl.ds(lo, n)], wd.at[b, pl.ds(0, n)], in_sems.at[b, 2]),
+        ]
+
+    def flush(j):
+        lo, n = FF_TILES[j]
+        b = j % 2
+        return [
+            pltpu.make_async_copy(gg.at[b, :, pl.ds(0, n)], g_gu.at[:, pl.ds(lo, n)], out_sems.at[b, 0]),
+            pltpu.make_async_copy(gup.at[b, :, pl.ds(0, n)], g_gu.at[:, pl.ds(ff + lo, n)], out_sems.at[b, 1]),
+            pltpu.make_async_copy(gd.at[b, pl.ds(0, n)], g_dn.at[pl.ds(lo, n)], out_sems.at[b, 2]),
+        ]
+
+    for copy in fetch(0):
+        copy.start()
+    x = tok[...].astype(F32)
+    resid = x + dot(mixed[...], wo[...])
+    normed, inverse = normalize(resid)
+    gain = gain_row(gains, 1)
+    h2_ref[...] = (normed * gain).astype(BF)
+    y_acc[...] = resid
+    for j, (lo, n) in enumerate(FF_TILES):
+        b = j % 2
+        for copy in fetch(j):
+            copy.wait()
+        if j + 1 < len(FF_TILES):
+            for copy in fetch(j + 1):
+                copy.start()
+        if j >= 2:
+            for copy in flush(j - 2):
+                copy.wait()
+        gate_w, up_w, down_w = wg[b, :, :n], wu[b, :, :n], wd[b, :n, :]
+        h2, dy = h2_ref[...], cot[...]
+        gate = dot(h2, gate_w)
+        up = dot(h2, up_w)
+        sig = jax.nn.sigmoid(gate)
+        silu = gate * sig
+        hid = (silu * up).astype(BF)
+        y_acc[...] += dot(hid, down_w)
+        gd[b, :n, :] = dot_l(hid, dy).astype(BF)
+        d_hid = dot_t(dy, down_w).astype(BF).astype(F32)
+        d_gate = (d_hid * up * sig * (1.0 + gate * (1.0 - sig))).astype(BF)
+        d_up = (d_hid * silu).astype(BF)
+        gg[b, :, :n] = dot_l(h2, d_gate).astype(BF)
+        gup[b, :, :n] = dot_l(h2, d_up).astype(BF)
+        term = dot_t(d_gate, gate_w) + dot_t(d_up, up_w)
+        if j == 0:
+            dh_acc[...] = term
+        else:
+            dh_acc[...] += term
+        for copy in flush(j):
+            copy.start()
+    out[...] = y_acc[...].astype(BF)
+    resid = tok[...].astype(F32) + dot(mixed[...], wo[...])
+    normed, inverse = normalize(resid)
+    dh = dh_acc[...]
+    g_gain[...] = jnp.sum(dh * normed, axis=0, keepdims=True)
+    back = cot[...].astype(F32) + norm_back(dh * gain, normed, inverse)
+    d_resid[...] = back
+    d_attn = back.astype(BF)
+    d_heads[...] = dot_t(d_attn, wo[...]).astype(BF)
+    g_wo[...] = dot_l(mixed[...], d_attn).astype(BF)
+    for j in (len(FF_TILES) - 2, len(FF_TILES) - 1):
+        for copy in flush(j):
+            copy.wait()
+
+
+def feed(tok, cot, mixed, wo, wl_full, gu, dn):
+    count = tok.shape[0]
+    whole = lambda *shape: pl.BlockSpec(shape, lambda i: (0,) * len(shape))
+    return pl.pallas_call(
+        feed_kernel,
+        name="feed",
+        grid=(1,),
+        in_specs=[
+            vmem(), vmem(), vmem(), vmem(),
+            pl.BlockSpec((1024, 128), lambda i: (0, 4)),
+            anywhere(), anywhere(),
+        ],
+        out_specs=[vmem(), vmem(), vmem(), vmem(), vmem(), anywhere(), anywhere()],
+        out_shape=[
+            jax.ShapeDtypeStruct((count, 1024), BF),
+            jax.ShapeDtypeStruct((count, 1024), F32),
+            jax.ShapeDtypeStruct((count, 1024), BF),
+            jax.ShapeDtypeStruct((1024, 1024), BF),
+            jax.ShapeDtypeStruct((1, 1024), F32),
+            jax.ShapeDtypeStruct(gu.shape, BF),
+            jax.ShapeDtypeStruct(dn.shape, BF),
+        ],
+        scratch_shapes=[
+            pltpu.VMEM((2, 1024, 768), BF),
+            pltpu.VMEM((2, 1024, 768), BF),
+            pltpu.VMEM((2, 768, 1024), BF),
+            pltpu.VMEM((2, 1024, 768), BF),
+            pltpu.VMEM((2, 1024, 768), BF),
+            pltpu.VMEM((2, 768, 1024), BF),
+            pltpu.VMEM((count, 1024), BF),
+            pltpu.VMEM((count, 1024), F32),
+            pltpu.VMEM((count, 1024), F32),
+            pltpu.SemaphoreType.DMA((2, 3)),
+            pltpu.SemaphoreType.DMA((2, 3)),
+        ],
+        compiler_params=pltpu.CompilerParams(vmem_limit_bytes=WIDE),
+    )(tok, cot, mixed, wo, wl_full, gu, dn)
+
+
+KEY_TILE = 1024
+GW, DN = [0, 1], [2]
+
+
+def attend_back_kernel(
+    q_ref, k_ref, v_ref, do_ref, o_ref, lse_ref, lim_ref, lat_ref, uk_ref, uv_ref, p_gu, p_wo, p_dn,
+    dq_ref, dlat_ref, guk_ref, guv_ref, t_gu, t_wo, t_dn,
+    dlat_acc, dk_all, dv_all, dq_acc, out_sems, *scratch,
+):
+    i = pl.program_id(0)
+    keys = k_ref.shape[0]
+    here = Place()
+    red = Reduce(
+        here, [p_gu, p_wo, p_dn], [CUTS["gu"], CUTS["wo"], CUTS["dn"]], ["plane", "plane", "line"], scratch
+    )
+
+    def meet_on(k, role):
+        return [lambda: red.meet(k, GW), lambda: red.line(k, GW, role)]
+
+    plan = {
+        (0, 0, 1): [lambda: red.pair(0), lambda: red.line(0, DN, 0)],
+        (0, 1, 0): [lambda: red.pair(1), lambda: red.line(1, DN, 0)],
+        (0, 1, 1): [lambda: red.pair(2), lambda: red.line(2, DN, 0)],
+        (1, 0, 0): [lambda: red.pair(3)],
+        (1, 1, 0): [lambda: red.turn(0, GW)],
+        (2, 0, 1): [lambda: red.turn(1, GW)],
+        (2, 1, 1): [lambda: red.line(0, DN, 1)],
+        (3, 0, 0): [lambda: red.turn(2, GW)],
+        (3, 1, 1): [lambda: red.turn(3, GW)],
+        (4, 0, 0): [lambda: red.meet(0, GW), lambda: red.line(0, GW, 0)],
+        (4, 1, 1): [lambda: red.line(1, DN, 1)],
+        (5, 0, 0): [lambda: red.line(2, DN, 1), lambda: red.meet(1, GW), lambda: red.line(1, GW, 0)],
+        (6, 0, 0): [lambda: red.line(0, GW, 1), lambda: red.meet(2, GW), lambda: red.line(2, GW, 0)],
+        (6, 1, 1): [lambda: red.line(3, DN), lambda: red.corner(2, 3)],
+        (7, 0, 1): [lambda: red.line(1, GW, 1)],
+        (7, 1, 0): [lambda: red.meet(3, GW)],
+        (7, 1, 1): [lambda: red.line(2, GW, 1), lambda: red.turn(3, DN)],
+    }
+
+    def at(tile, h):
+        for (step, part, head), acts in plan.items():
+            if head == h:
+
+                @pl.when(jnp.logical_and(i == step, tile == part))
+                def _():
+                    for act in acts:
+                        act()
+
+    @pl.when(i == 0)
+    def _():
+        here.greet()
+        red.start()
+
+    deltas = []
+    for h in range(2):
+        cs = slice(64 * h, 64 * h + 64)
+        prod = do_ref[:, cs].astype(F32) * o_ref[:, cs].astype(F32)
+        deltas.append(jnp.sum(prod.T, axis=0, keepdims=True))
+    dq_acc[...] = jnp.zeros_like(dq_acc)
+
+    @pl.loop(0, keys // KEY_TILE)
+    def _(t):
+        rows = pl.ds(pl.multiple_of(t * KEY_TILE, KEY_TILE), KEY_TILE)
+        d_keys, d_values = [], []
+        for h in range(2):
+            at(t, h)
+            cs = slice(64 * h, 64 * h + 64)
+            q = q_ref[:, cs] * jnp.asarray(0.125, BF)
+            d_out = do_ref[:, cs]
+            key, value = k_ref[rows, cs], v_ref[rows, cs]
+            scores = dot_t(key, q)
+            place = lax.broadcasted_iota(jnp.int32, scores.shape, 0) + t * KEY_TILE
+            probs = jnp.where(place < lim_ref[...], jnp.exp(scores - lse_ref[0, h : h + 1, :]), 0.0)
+            d_probs = dot_t(value, d_out)
+            d_scores = (probs * (d_probs - deltas[h])).astype(BF)
+            d_values.append(dot(probs.astype(BF), d_out))
+            d_keys.append(dot(d_scores, q))
+            dq_acc[:, cs] += dot_l(d_scores, key)
+        dk_all[rows, :] = jnp.concatenate(d_keys, axis=1).astype(BF)
+        dv_all[rows, :] = jnp.concatenate(d_values, axis=1).astype(BF)
+
+    dq_ref[...] = (dq_acc[...] * 0.125).astype(BF)
+    d_key, d_value = dk_all[...], dv_all[...]
+    latents = lat_ref[0]
+    guk_ref[...] = dot_l(latents, d_key).astype(BF)
+    guv_ref[...] = dot_l(latents, d_value).astype(BF)
+    term = dot_t(d_key, uk_ref[...]) + dot_t(d_value, uv_ref[...])
+
+    @pl.when(lax.rem(i, 4) == 0)
+    def _():
+        dlat_acc[...] = term
+
+    @pl.when(lax.rem(i, 4) != 0)
+    def _():
+        dlat_acc[...] += term
+
+    @pl.when(lax.rem(i, 4) == 3)
+    def _():
+        dlat_ref[0] = dlat_acc[...].astype(BF)
+
+    @pl.when(i == 7)
+    def _():
+        red.line(3, GW)
+        red.meet(3, DN)
+        copies = [
+            pltpu.make_async_copy(red.result(t), out, out_sems.at[t])
+            for t, out in enumerate((t_gu, t_wo, t_dn))
+        ]
+        for copy in copies:
+            copy.start()
+        red.drain()
+        for copy in copies:
+            copy.wait()
+
+
+def attend_back(q, k, v, d_heads, mixed, lse, limits, lat_full, u_full, parts, collective_id):
+    count, keys = q.shape[0], lat_full.shape[1]
+    wide = pl.BlockSpec((count, 128), lambda i: (0, i))
+    tall = pl.BlockSpec((keys, 128), lambda i: (0, i))
+    return pl.pallas_call(
+        attend_back_kernel,
+        name="attend_back",
+        grid=(8,),
+        in_specs=[
+            wide, tall, tall, wide, wide,
+            pl.BlockSpec((1, 2, count), lambda i: (i, 0, 0)),
+            pl.BlockSpec((1, count), lambda i: (0, 0)),
+            pl.BlockSpec((1, keys, 256), lambda i: (i // 4, 0, 0)),
+            pl.BlockSpec((256, 128), lambda i: (0, i)),
+            pl.BlockSpec((256, 128), lambda i: (0, 8 + i)),
+            anywhere(), anywhere(), anywhere(),
+        ],
+        out_specs=[
+            wide,
+            pl.BlockSpec((1, keys, 256), lambda i: (i // 4, 0, 0)),
+            pl.BlockSpec((256, 128), lambda i: (0, i)),
+            pl.BlockSpec((256, 128), lambda i: (0, i)),
+            anywhere(), anywhere(), anywhere(),
+        ],
+        out_shape=[
+            jax.ShapeDtypeStruct((count, 1024), BF),
+            jax.ShapeDtypeStruct((2, keys, 256), BF),
+            jax.ShapeDtypeStruct((256, 1024), BF),
+            jax.ShapeDtypeStruct((256, 1024), BF),
+        ]
+        + [jax.ShapeDtypeStruct(a.shape[2:], BF) for a in parts],
+        scratch_shapes=[
+            pltpu.VMEM((keys, 256), F32),
+            pltpu.VMEM((keys, 128), BF),
+            pltpu.VMEM((keys, 128), BF),
+            pltpu.VMEM((count, 128), F32),
+            pltpu.SemaphoreType.DMA((3,)),
+        ]
+        + Reduce.scratch(
+            [a.shape[2:] for a in parts],
+            [CUTS["gu"], CUTS["wo"], CUTS["dn"]],
+            ["plane", "plane", "line"],
+        ),
+        compiler_params=pltpu.CompilerParams(
+            collective_id=collective_id, has_side_effects=True, vmem_limit_bytes=WIDE
+        ),
+    )(q, k, v, d_heads, mixed, lse, limits, lat_full, u_full, u_full, *parts)
+
+
+LATE_CUTS = [8, 8, 16, 16]
+LATE_WAYS = ["plane"] * 4
+
+
+def close_kernel(
+    tok, wq, wl, d_resid, dq, g_gain2, dlat, p_uk, p_uv, t_gu, t_wo, t_dn,
+    g_tok, o_gu, o_wo, o_dn, o_uk, o_uv, o_wq, o_wl,
+    mine, da, db, xb, yb, dh_acc, g_wq, g_wl, sends, recvs, locals_,
+    a_send, a_recv, a_loc, b_send, b_recv, b_loc, *scratch,
+):
+    here = Place()
+    s, xs, ys, ds, f = here.s, here.xs, here.ys, here.ds, here.f
+    count = tok.shape[0]
+    half = count // 2
+    red = Reduce(here, [p_uk, p_uv, g_wq, g_wl], LATE_CUTS, LATE_WAYS, scratch)
+    early = Share(
+        here, [t_gu, t_wo, t_dn], [o_gu, o_wo, o_dn], [CUTS["gu"], CUTS["wo"], CUTS["dn"]],
+        a_send, a_recv, a_loc,
+    )
+    late = Share(
+        here, [red.result(t) for t in range(4)], [o_uk, o_uv, o_wq, o_wl], LATE_CUTS,
+        b_send, b_recv, b_loc,
+    )
+    w = Wire(sends, recvs, 0)
+    load = pltpu.make_async_copy(dlat, mine, locals_.at[0])
+
+    def corners():
+        w.send(0, dlat.at[:, ds, pl.ds(0, half)], da, (ys, f))
+        w.send(1, dlat.at[:, ds, pl.ds(half, half)], db, (xs, f))
+
+    def sides():
+        w.send(2, mine.at[:, xs], xb, (xs, f))
+        w.send(3, mine.at[:, ys], yb, (ys, f))
+
+    here.greet()
+    load.start()
+    corners()
+    red.start([0, 1])
+    normed, inverse = normalize(tok[...].astype(F32))
+    gain = gain_row(wl[:, 512:], 0)
+    h1 = (normed * gain).astype(BF)
+    g_wq[...] = dot_l(h1, dq[...]).astype(BF).reshape(g_wq.shape)
+    red.start([2])
+    load.wait()
+    w.recv(0, da, (ys, f))
+    w.recv(1, db, (xs, f))
+    for g in range(2):
+        add_into(mine.at[g, xs, pl.ds(0, half)], [da.at[g]])
+        add_into(mine.at[g, ys, pl.ds(half, half)], [db.at[g]])
+    sides()
+    dh_acc[...] = dot_t(dq[...], wq[...])
+    for i in range(4):
+        red.pair(i, [0, 1])
+    for i in range(4):
+        red.pair(i, [2])
+    early.start()
+    w.recv(2, xb, (xs, f))
+    w.recv(3, yb, (ys, f))
+    dh = dh_acc[...]
+    halves = []
+    for g in range(2):
+        total = mine[g, s].astype(F32) + xb[g].astype(F32) + yb[g].astype(F32)
+        d_lat = total.astype(BF)
+        cols = slice(256 * g, 256 * g + 256)
+        g_wl[:, :, :, cols] = dot_l(h1, d_lat).astype(BF).reshape(8, 4, 32, 256)
+        dh = dh + dot_t(d_lat, wl[:, cols])
+    g_gain1 = jnp.sum(dh * normed, axis=0, keepdims=True)
+    g_wl[:, :, :, 512:] = jnp.zeros((8, 4, 32, 128), BF)
+    for k in range(8):
+        cols = slice(128 * k, 128 * k + 128)
+        rows = [g_gain1[:, cols], g_gain2[:, cols], jnp.zeros((14, 128), F32)]
+        g_wl[k, 0, :16, 512:] = jnp.concatenate(rows, axis=0).astype(BF)
+    red.start([3])
+    g_tok[...] = d_resid[...] + norm_back(dh * gain, normed, inverse)
+    for i in range(4):
+        red.turn(i, [0, 1, 2])
+    for i in range(4):
+        red.pair(i, [3])
+    early.turn()
+    for i in range(4):
+        red.turn(i, [3])
+    for i in range(3):
+        red.meet(i)
+        red.line(i, None, 0)
+    for i in range(3):
+        red.line(i, None, 1)
+    red.meet(3)
+    red.line(3)
+    late.start()
+    early.arrive()
+    late.turn()
+    late.arrive()
+    w.draining = True
+    corners()
+    sides()
+    red.drain()
+    early.drain()
+    late.drain()
+
+
+def close(tok, wq, wl, d_resid, dq, g_gain2, dlat, parts, quarters, collective_id):
+    count = tok.shape[0]
+    wide = lambda q, c: jax.ShapeDtypeStruct((4, q, c), BF)
+    shapes = [(8, 1024), (8, 1024), (32, 1024), (32, 640)]
+    return pl.pallas_call(
+        close_kernel,
+        name="close",
+        in_specs=[vmem()] * 6 + [anywhere()] * 6,
+        out_specs=[vmem()] + [anywhere()] * 7,
+        out_shape=[jax.ShapeDtypeStruct((count, 1024), F32)]
+        + [wide(*a.shape) for a in quarters]
+        + [wide(*a) for a in shapes],
+        scratch_shapes=[
+            pltpu.VMEM((2, 4, count, 256), BF),
+            pltpu.VMEM((2, count // 2, 256), BF),
+            pltpu.VMEM((2, count // 2, 256), BF),
+            pltpu.VMEM((2, count, 256), BF),
+            pltpu.VMEM((2, count, 256), BF),
+            pltpu.VMEM((count, 1024), F32),
+            pltpu.VMEM((8, 4, 32, 1024), BF),
+            pltpu.VMEM((8, 4, 32, 640), BF),
+            pltpu.SemaphoreType.DMA((1, 4)),
+            pltpu.SemaphoreType.DMA((1, 4)),
+            pltpu.SemaphoreType.DMA((1,)),
+        ]
+        + Share.sems(3)
+        + Share.sems(4)
+        + Reduce.scratch(shapes, LATE_CUTS, LATE_WAYS),
+        compiler_params=pltpu.CompilerParams(
+            collective_id=collective_id, has_side_effects=True, vmem_limit_bytes=WIDE
+        ),
+    )(tok, wq, wl, d_resid, dq, g_gain2, dlat, *parts, *quarters)
+
+
+def eighths(array):
+    rows, cols = array.shape
+    return array.reshape(8, 4, rows // 32, cols)
+
+
+def flat(array):
+    return array.reshape(-1, array.shape[-1])
+
+
+def fast_local(
+    tokens, block_ids, gain_attn, w_query, w_latent, up_key, up_value, w_out,
+    gain_ffn, w_gate, w_up, w_down, cotangent,
+):
+    count = tokens.shape[1]
+    x, dy = tokens[0], cotangent[0]
+    gains = jnp.concatenate([gain_attn[None], gain_ffn[None], jnp.zeros((126, 128), BF)])
+    wl = jnp.concatenate([w_latent, gains], axis=1)
+    u = jnp.concatenate(
+        [
+            up_key.transpose(1, 0, 2).reshape(32, 1024),
+            up_value.transpose(1, 0, 2).reshape(32, 1024),
+        ],
+        axis=1,
+    )
+    gu = jnp.concatenate([w_gate, w_up], axis=1)
+    ids = block_ids[0]
+    own = lax.dynamic_slice_in_dim(ids, lax.axis_index("seq") * count, count)
+    limits = jnp.sum((ids[:, None] <= own[None, :]).astype(jnp.int32), axis=0, keepdims=True)
+    mixed, lse, k, v, q, lat, wl_full, wq_full, u_full, gu_full, dn_full, wo_full = open_call(
+        x, limits, wl, w_query, u, gu, w_down, w_out, 0
+    )
+    lat_full = lat.reshape(GROUPS, 4 * count, LATENT)
+    out, d_resid, d_heads, g_wo, g_gain2, g_gu, g_dn = feed(
+        x, dy, mixed, wo_full, wl_full, gu_full, dn_full
+    )
+    parts = [eighths(a) for a in (g_gu, g_wo, g_dn)]
+    dq, dlat, g_uk, g_uv, t_gu, t_wo, t_dn = attend_back(
+        q, k, v, d_heads, mixed, lse, limits, lat_full, u_full, parts, 1
+    )
+    d_tokens, *shards = close(
+        x, wq_full, wl_full, d_resid, dq, g_gain2, dlat.reshape(GROUPS, 4, count, LATENT),
+        [eighths(g_uk), eighths(g_uv)], [t_gu, t_wo, t_dn], 2,
+    )
+    r_gu, r_wo, r_dn, r_uk, r_uv, r_wq, r_wl = (flat(a).astype(F32) for a in shards)
+    lift = lambda a: a.reshape(32, GROUPS, 512).transpose(1, 0, 2)
+    return (
+        out[None],
+        d_tokens[None],
+        r_wl[0, 512:],
+        r_wq,
+        r_wl[:, :512],
+        lift(r_uk),
+        lift(r_uv),
+        r_wo,
+        r_wl[1, 512:],
+        r_gu[:, :2816],
+        r_gu[:, 2816:],
+        r_dn,
+    )
+
+
 def solution(mesh):
     placed = (
         P("fsdp", "seq", None),
@@ -302,8 +1468,9 @@
         P("fsdp", None),
         P("fsdp", "seq", None),
     )
+    tuned = (mesh.shape["seq"], mesh.shape["fsdp"]) == (4, 8)
     return jax.shard_map(
-        local,
+        fast_local if tuned else local,
         mesh=mesh,
         in_specs=placed,
         out_specs=(

time: 1200 us -> 388 us (0.32)
  waiting for transfers between devices: 678 us -> 0 us
  Pallas kernels: 0 us -> 359 us
  matrix products: 346 us -> 0 us
  blocking collectives: 79.9 us -> 0 us
  other arithmetic: 39.3 us -> 10.4 us
  local copies, waits for them, and re-layouts: 30.2 us -> 10.4 us
  between operations: 15.2 us -> 0.98 us
    reduce_scatter x10 -> x0, waiting for transfers between devices: 431 us -> none  [the longest x1 65.4 us: local(): lax.psum_scatter(grad_down.astype(jnp.bfloat16), 'fsdp', scatter_dimensio...]
    pallas_call x0 -> x4, Pallas kernels: none -> 359 us  [the longest x1 124 us: open_call(): pl.pallas_call(open_kernel, name='open', grid=(8,), in_specs=[pl.BlockSpe...]
    dot_general x136 -> x0, matrix products: 346 us -> none  [the longest x32 75.7 us: masked_scores(): jnp.einsum('qd,kd->qk', query_head, key_head, preferred_element_type=jnp....]
    all_gather x8 -> x0, waiting for transfers between devices: 196 us -> none  [the longest x1 52.5 us: local(): lax.all_gather(w_gate, 'fsdp', axis=0, tiled=True)]
    all_gather x4 -> x0, blocking collectives: 56.2 us -> none  [the longest x1 17 us: local(): lax.all_gather(up_value, 'fsdp', axis=1, tiled=True)]
    psum x1 -> x0, waiting for transfers between devices: 46.4 us -> none  [local(): lax.psum(part_query.astype(jnp.bfloat16), 'seq').astype(jnp.float32)]
    unnamed x54 -> x11, local copies, waits for them, and re-layouts: 25 us -> 2.2 us
    convert_element_type x29 -> x4, other arithmetic: 22.3 us -> 3.73 us  [fast_local(): flat(a).astype(F32)]
  transfers between devices with their start and end apart: 19 -> 0, of which waited for: 15 -> 0; matrix products, arithmetic and copies ran while one was open for 16% -> 0% of each run, Pallas kernels for 0% -> 0%
where the time goes in v2:
time: 388 us; the launch traced here: 381 us
  Pallas kernels  359 us (93%)
  local copies, waits for them, and re-layouts  10.4 us (3%)
  other arithmetic  10.4 us (3%)
    pallas_call x1, Pallas kernels, open_call(): pl.pallas_call(open_kernel, name='open', grid=(8,), in_specs=[pl.BlockSpe...  124 us
    pallas_call x1, Pallas kernels, attend_back(): pl.pallas_call(attend_back_kernel, name='attend_back', grid=(8,), in_spec...  102 us
    pallas_call x1, Pallas kernels, close(): pl.pallas_call(close_kernel, name='close', in_specs=[vmem()] * 6 + [anywh...  85.7 us
    pallas_call x1, Pallas kernels, feed(): pl.pallas_call(feed_kernel, name='feed', grid=(1,), in_specs=[vmem(), vme...  46.6 us

profile of v2, /device:TPU:0, one launch (start us, length us, event | category | flops | bytes accessed | tf_op | source)
XLA Modules:
  0.0 380.6 jit_solution(3875138336361691297)
XLA Ops:
  0.6 0.7 constant_dynamic-slice_fusion
  1.3 1.8 convert_reduce_fusion
  3.2 0.8 copy.33
  4.0 0.8 copy.34
  4.9 0.7 pad_maximum_fusion.1.u_s
  5.5 1.6 maximum_maximum_fusion.wl_s
  7.1 2.5 pad_maximum_fusion.gu_s
  9.7 124.5 %open.1 = (bf16[512,1024]{1,0:T(8,128)(2,1)}, f32[8,2,512]{2,1,0:T(2,128)}, bf16[2048,1024]{1,0:T(8,128)(2,1)}, bf16[2048,1024]{1,0:T(8,128)(2,1)}, bf16[512,102...) custom-call(bf16[512,1024]{1,0:T(8,128)(2,1)} %bitcast.46, ...), custom_call_target="tpu_custom_call" | custom-call | tf_op jit(solution)/shard_map/open/pallas_call | solution.py:926
  134.2 46.6 %feed.1 = (bf16[512,1024]{1,0:T(8,128)(2,1)}, f32[512,1024]{1,0:T(8,128)}, bf16[512,1024]{1,0:T(8,128)(2,1)}, bf16[1024,1024]{1,0:T(8,128)(2,1)}, f32[1,1024]{1,...) custom-call(bf16[512,1024]{1,0:T(8,128)(2,1)} %bitcast.47, bf16[512,1024]{1,0:T(8,128)(2,1)} %bitcast.54, ...), custom_call_target="tpu_custom_call" | custom-call | tf_op jit(solution)/shard_map/feed/pallas_call | solution.py:1060
  180.8 102.1 %attend_back.1 = (bf16[512,1024]{1,0:T(8,128)(2,1)}, bf16[2,2048,256]{2,1,0:T(8,128)(2,1)}, bf16[256,1024]{1,0:T(8,128)(2,1)}, bf16[256,1024]{1,0:T(8,128)(2,1)}...) custom-call(bf16[512,1024]{1,0:T(8,128)(2,1)} %get-tuple-element.54.q_ref, ...), custom_call_target="tpu_custom_call" | custom-call | tf_op jit(solution)/shard_map/attend_back/pallas_call | solution.py:1215
  282.9 85.7 %close.1 = (f32[512,1024]{1,0:T(8,128)}, bf16[4,32,5632]{2,1,0:T(8,128)(2,1)}, bf16[4,32,1024]{2,1,0:T(8,128)(2,1)}, bf16[4,88,1024]{2,1,0:T(8,128)(2,1)}, bf16[...) custom-call(bf16[512,1024]{1,0:T(8,128)(2,1)} %bitcast.48, ...), custom_call_target="tpu_custom_call" | custom-call | tf_op jit(solution)/shard_map/close/pallas_call | solution.py:1364
  368.5 0.0 copy-start.3
  368.6 0.0 copy-start.4
  368.6 0.0 copy-start.2
  368.6 1.1 reshape.93
  369.6 1.0 reshape.94
  370.6 0.8 copy_bitcast_fusion
  371.4 0.9 bitcast_convert_fusion.4
  372.3 0.5 slice_bitcast_fusion
  372.8 0.0 copy-start.1
  372.8 0.7 slice.21
  373.6 0.0 copy-done.3
  373.6 0.0 copy-done.4
  373.6 1.1 bitcast_convert_fusion.2
  374.7 0.0 copy-done.2
  374.7 1.3 bitcast_convert_fusion.1
  376.0 0.0 copy-done.1
  376.0 0.4 bitcast_convert_fusion
  376.4 0.0 copy-start
  376.4 1.8 fusion
  378.1 0.9 copy-done
  379.0 1.3 copy.38
  (1 shorter events, 0.0 us)
Async XLA Ops:
  368.5 5.0 %copy-start.3 = (bf16[4,32,1024]{2,1,0:T(8,128)(2,1)S(1)}, bf16[4,32,1024]{2,1,0:T(8,128)(2,1)}, u32[]{:S(2)}) copy-start(bf16[4,32,1024]{2,1,0:T(8,128)(2,1)} %get-tuple-element.77) | copy-start | bytes 786436
  368.6 5.0 %copy-start.4 = (bf16[4,32,1024]{2,1,0:T(8,128)(2,1)S(1)}, bf16[4,32,1024]{2,1,0:T(8,128)(2,1)}, u32[]{:S(2)}) copy-start(bf16[4,32,1024]{2,1,0:T(8,128)(2,1)} %get-tuple-element.74) | copy-start | bytes 786436
  368.6 6.1 %copy-start.2 = (bf16[4,88,1024]{2,1,0:T(8,128)(2,1)S(1)}, bf16[4,88,1024]{2,1,0:T(8,128)(2,1)}, u32[]{:S(2)}) copy-start(bf16[4,88,1024]{2,1,0:T(8,128)(2,1)} %get-tuple-element.79) | copy-start | bytes 2162692
  372.8 3.2 copy-start.1
  376.4 2.6 copy-start
